TPU v7x, 32 devices: a whole 2x2x4 slice. The times are simulated.
32 devices in a mesh: lon: 4 (over y, core), lat: 8 (over z, x).
Axes of the slice: x: 2, y: 2, z: 4, core: 2. Of those that a mesh axis runs over, the one named last changes fastest.
Arguments:
- thermal_deviation: float32 [32, 32, 512], P(None, 'lat', 'lon'), may hold values from -5 to 5
- moisture_deviation: float32 [32, 32, 512], P(None, 'lat', 'lon'), may hold values from -5 to 5
- eastward_stability: float32 [32, 32, 512], P(None, 'lat', 'lon'), may hold values from -0.5 to 0.5
- northward_stability: float32 [32, 32, 512], P(None, 'lat', 'lon'), may hold values from -0.4 to 0.4
- sun_height_ratio: float32 [32, 512], P('lat', 'lon'), may hold values from 0.25 to 1
- extinction_coeff: float32 [112, 32], replicated, may hold values from 0.005 to 0.05
- reflectivity_ratio: float32 [112], replicated, may hold values from 0.1 to 0.9
- insolation_source: float32 [112], replicated, may hold values from 0.05 to 0.5
- daylight_tally: int32 [8, 4], P('lat', 'lon'), may hold values from 0 to 512, as said below
- daylight_permutation: int32 [8, 4, 512], P('lat', 'lon'), may hold values from 0 to 511, as said below
Outputs:
- temperature_next: float32 [32, 32, 512], P(None, 'lat', 'lon')
- humidity_next: float32 [32, 32, 512], P(None, 'lat', 'lon')
- warming_tendency: float32 [32, 32, 512], P(None, 'lat', 'lon')
Inputs may be any that keep to these rules, and one draw needn't show every extreme that they name: `daylight_tally`: the block at longitude block j and the one at j + 2 in the same latitude band together have exactly 512 sunlit columns; some block has all 512 sunlit and some has none. `daylight_permutation`: each block's list is an ordering of its 512 local column indices; its first entries, as many as the block's sunlit count, are its sunlit columns.
All inputs are finite; a program needn't handle non-finite values.
Results may differ from a plain program's by a relative error of at most 0.0003.
Values sent between devices are 32-bit elements; how exact they have to be, the bound alone decides.
No kernel may reach another device: no remote copies, remote signals or barrier semaphores. Data moves between devices by JAX's collectives and lax.ppermute only.
A program may use at most 64 MiB of HBM per device.

v0:
```python
import jax
import jax.numpy as jnp
from jax import lax
from jax.sharding import PartitionSpec as P

heat_coeff = 20.0


def passed_along(array, axis, by):
    length = lax.axis_size(axis)
    return lax.ppermute(array, axis, [(i, (i + by) % length) for i in range(length)])


def extended(block, sides, width):
    for axis, dim in sides:
        count = lax.axis_size(axis)
        forward = [(i, i + 1) for i in range(count - 1)]
        forward.append((count - 1, 0))
        backward = [(target, source) for source, target in forward]
        low = lax.ppermute(
            lax.slice_in_dim(block, block.shape[dim] - width, None, axis=dim), axis, forward
        )
        high = lax.ppermute(lax.slice_in_dim(block, 0, width, axis=dim), axis, backward)
        block = jnp.concatenate([low, block, high], axis=dim)
    return block


def cyclic(sub_band, main_band, super_band, rhs_band):
    if rhs_band.shape[0] == 1:
        return rhs_band / main_band
    even_sub, odd_sub = (sub_band[0::2], sub_band[1::2])
    even_main, odd_main = (main_band[0::2], main_band[1::2])
    even_super, odd_super = (super_band[0::2], super_band[1::2])
    even_rhs, odd_rhs = (rhs_band[0::2], rhs_band[1::2])
    edge_zero = jnp.zeros_like(rhs_band[:1])
    edge_one = jnp.ones_like(rhs_band[:1])
    next_sub = jnp.concatenate([even_sub[1:], edge_zero], axis=0)
    next_main = jnp.concatenate([even_main[1:], edge_one], axis=0)
    next_super = jnp.concatenate([even_super[1:], edge_zero], axis=0)
    next_rhs = jnp.concatenate([even_rhs[1:], edge_zero], axis=0)
    alpha_term = -odd_sub / even_main
    gamma_term = -odd_super / next_main
    odd_values = cyclic(
        alpha_term * even_sub,
        odd_main + alpha_term * even_super + gamma_term * next_sub,
        gamma_term * next_super,
        odd_rhs + alpha_term * even_rhs + gamma_term * next_rhs,
    )
    left_values = jnp.concatenate([edge_zero, odd_values[:-1]], axis=0)
    even_values = (even_rhs - even_sub * left_values - even_super * odd_values) / even_main
    return jnp.stack([even_values, odd_values], axis=1).reshape(rhs_band.shape)


def column_heating(
    temp_cols, hum_cols, cos_cols, extinction_coeff, reflectivity_ratio, insolation_source
):
    stratum_group = temp_cols.shape[0]
    factor = (1.5 + jnp.tanh(hum_cols)) * (1.0 + 0.25 * jnp.tanh(temp_cols))
    gblock = 16
    count_blocks = extinction_coeff.shape[0] // gblock
    blocks = (
        extinction_coeff.reshape(count_blocks, gblock, stratum_group),
        reflectivity_ratio.reshape(count_blocks, gblock),
        insolation_source.reshape(count_blocks, gblock),
    )

    def one_block(block):
        block_absorb, block_albedo, block_solar = block
        optical = jnp.transpose(block_absorb)[:, :, None] * factor[:, None, :]
        path_depth = jnp.cumsum(optical, axis=0) - 0.5 * optical
        direct = (
            block_solar[None, :, None]
            * cos_cols[None, None, :]
            * jnp.exp(-path_depth / cos_cols[None, None, :])
        )
        source = block_albedo[None, :, None] * direct
        coupling = 2.0 / (1.0 + 3.0 * (optical[:-1] + optical[1:]))
        edge_row = jnp.zeros_like(optical[:1])
        upper_band = jnp.concatenate([coupling, edge_row], axis=0)
        lower_band = jnp.concatenate([edge_row, coupling], axis=0)
        absorbed = (1.0 - block_albedo)[None, :, None] * optical
        diagonal = 0.5 + upper_band + lower_band + absorbed
        diffuse = cyclic(-lower_band, diagonal, -upper_band, source)
        return jnp.sum(absorbed * (diffuse + direct), axis=1)

    return heat_coeff * jnp.sum(lax.map(one_block, blocks), axis=0)


def fix_rims(padded, depth):
    lat_index = lax.axis_index("lat")
    lat_count = lax.axis_size("lat")
    rows = padded.shape[2]
    row_ids = jnp.arange(rows, dtype=jnp.int32)
    source_rows = jnp.where((row_ids < depth) & (lat_index == 0), depth, row_ids)
    source_rows = jnp.where(
        (row_ids >= rows - depth) & (lat_index == lat_count - 1), rows - depth - 1, source_rows
    )
    return jnp.take(padded, source_rows, axis=2)


def stencil(padded, courant_x, courant_y):
    quantity_group = padded[:, :, 1:-1, 1:-1]
    eastern = padded[:, :, 1:-1, 2:]
    western = padded[:, :, 1:-1, :-2]
    northern = padded[:, :, 2:, 1:-1]
    southern = padded[:, :, :-2, 1:-1]
    return (
        quantity_group
        - 0.5 * courant_x * (eastern - western)
        + 0.5 * courant_x * courant_x * (eastern - 2.0 * quantity_group + western)
        - 0.5 * courant_y * (northern - southern)
        + 0.5 * courant_y * courant_y * (northern - 2.0 * quantity_group + southern)
    )


def local(
    thermal_deviation,
    moisture_deviation,
    eastward_stability,
    northward_stability,
    sun_height_ratio,
    extinction_coeff,
    reflectivity_ratio,
    insolation_source,
    daylight_tally,
    daylight_permutation,
):
    quantity_group = jnp.stack([thermal_deviation, moisture_deviation])
    stratum_group = thermal_deviation.shape[0]
    profile_group = thermal_deviation.shape[1] * thermal_deviation.shape[2]
    halfway = profile_group // 2
    listing = daylight_permutation.reshape(profile_group)
    state = quantity_group.reshape(2, stratum_group, profile_group)
    own_state = jnp.take(state, listing, axis=2)
    own_cos = jnp.take(sun_height_ratio.reshape(profile_group), listing)
    own_count = daylight_tally[0, 0]
    lon_count = lax.axis_size("lon")
    lon_index = lax.axis_index("lon")
    is_first = lon_index < lon_count // 2
    first_count = jnp.where(is_first, own_count, profile_group - own_count)
    slots = jnp.arange(profile_group, dtype=jnp.int32)
    shares = jnp.arange(halfway, dtype=jnp.int32)
    peer_state, peer_cos = passed_along((own_state, own_cos), "lon", lon_count // 2)
    places = jnp.where(is_first, shares, halfway + shares)
    from_first = places < first_count
    first_state = jnp.where(is_first, own_state, peer_state)
    second_state = jnp.where(is_first, peer_state, own_state)
    first_cos = jnp.where(is_first, own_cos, peer_cos)
    second_cos = jnp.where(is_first, peer_cos, own_cos)
    first_pos = jnp.clip(places, 0, profile_group - 1)
    second_pos = jnp.clip(places - first_count, 0, profile_group - 1)
    work_state = jnp.where(
        from_first,
        jnp.take(first_state, first_pos, axis=2),
        jnp.take(second_state, second_pos, axis=2),
    )
    work_cos = jnp.where(
        from_first, jnp.take(first_cos, first_pos), jnp.take(second_cos, second_pos)
    )
    work_heat = column_heating(
        work_state[0],
        work_state[1],
        work_cos,
        extinction_coeff,
        reflectivity_ratio,
        insolation_source,
    )
    peer_heat = passed_along(work_heat, "lon", lon_count // 2)
    joined = jnp.where(
        is_first,
        jnp.concatenate([work_heat, peer_heat], axis=1),
        jnp.concatenate([peer_heat, work_heat], axis=1),
    )
    positions = jnp.clip(jnp.where(is_first, slots, first_count + slots), 0, profile_group - 1)
    position_warming = jnp.take(joined, positions, axis=1)
    position_warming = jnp.where(slots[None, :] < own_count, position_warming, 0.0)
    partition_identifiers = jnp.zeros((profile_group,), jnp.int32).at[listing].set(slots)
    warming_tendency = jnp.take(position_warming, partition_identifiers, axis=1).reshape(
        thermal_deviation.shape
    )
    stacked = jnp.concatenate(
        [quantity_group, eastward_stability[None], northward_stability[None]], axis=0
    )
    padded = extended(stacked, (("lat", 2), ("lon", 3)), 2)
    first_step = stencil(
        fix_rims(padded[:2], 2), padded[2, :, 1:-1, 1:-1], padded[3, :, 1:-1, 1:-1]
    )
    quantity_group = stencil(fix_rims(first_step, 1), eastward_stability, northward_stability)
    return (quantity_group[0], quantity_group[1], warming_tendency)


def solution(mesh):
    placed = (
        P(None, "lat", "lon"),
        P(None, "lat", "lon"),
        P(None, "lat", "lon"),
        P(None, "lat", "lon"),
        P("lat", "lon"),
        P(),
        P(),
        P(),
        P("lat", "lon"),
        P("lat", "lon", None),
    )
    return jax.shard_map(
        local,
        mesh=mesh,
        in_specs=placed,
        out_specs=(P(None, "lat", "lon"), P(None, "lat", "lon"), P(None, "lat", "lon")),
        check_vma=False,
    )
```

profile of v0, /device:TPU:1, one launch (start us, length us, event | category | flops | bytes accessed | tf_op | source)
XLA Modules:
  0.0 115.6 jit_solution(7224442794884020200)
XLA Ops:
  1.4 3.5 %gather_fusion.3 = f32[512]{0:T(512)S(1)} fusion(f32[512]{0:T(512)S(1)} %bitcast.138, s32[1024]{0:T(1024)S(1)} %pad_clamp_fusion.4), kind=kCustom, calls=%fused_computation.9 | custom fusion | bytes 6144 | tf_op jit(solution)/shard_map/jit(_take)/gather | solution.py:135
  4.9 2.1 %collective-permute-start.5 = (f32[512]{0:T(512)S(1)}, f32[512]{0:T(512)S(1)}, u32[]{:S(2)}, u32[]{:S(2)}) collective-permute-start(f32[512]{0:T(512)S(1)} %get-tuple-element.98), channel_id=1, source_target_pairs={{0,16},{8,24},{16,0},{24,8},{1,17},{9,25},{17,1},{25,9},{2,18},{10... | collective-permute-start | bytes 6152 | tf_op jit(solution)/shard_map/ppermute | solution.py:11
  7.4 2.1 %gather_fusion.2 = f32[512,2,32]{2,1,0:T(2,128)S(1)} fusion(f32[2,32,512]{1,0,2:T(2,128)S(1)} %copy.80, s32[1024]{0:T(1024)S(1)} %pad_clamp_fusion.4), kind=kCustom, calls=%fused_computation.8 | custom fusion | bytes 264192 | tf_op jit(solution)/shard_map/jit(_take)/gather | solution.py:134
  9.5 1.8 %select_bitcast_fusion = f32[2,32,512]{1,0,2:T(2,128)S(1)} fusion(f32[512,2,32]{2,1,0:T(2,128)S(1)} %gather_fusion.2, pred[512]{0:T(512)(128)(4,1)S(1)} %get-tuple-element.99), kind=kLoop, calls=%fused_computation.93 | loop fusion | flops 32768 | bytes 262656 | tf_op jit(solution)/shard_map/jit(_take)/select_n | solution.py:134
  12.2 1.3 %collective-permute-start = (f32[4,32,2,128]{3,1,2,0:T(8,128)S(1)}, f32[4,32,2,128]{3,1,2,0:T(8,128)S(1)}, u32[]{:S(2)}, u32[]{:S(2)}) collective-permute-start(f32[4,32,2,128]{3,1,2,0:T(8,128)S(1)} %get-tuple-element.129), channel_id=1, source_target_pairs={{0,1},{1,2},{2,3},{3,4},{4,5},{5,6},{6,7},{7,0},{8,9},{9,10},{10,1... | collective-permute-start | bytes 393224 | tf_op jit(solution)/shard_map/ppermute | solution.py:20
  13.4 3.1 %collective-permute-start.1 = (f32[4,32,2,128]{3,1,2,0:T(8,128)S(1)}, f32[4,32,2,128]{3,1,2,0:T(8,128)S(1)}, u32[]{:S(2)}, u32[]{:S(2)}) collective-permute-start(f32[4,32,2,128]{3,1,2,0:T(8,128)S(1)} %get-tuple-element.130), channel_id=1, source_target_pairs={{1,0},{2,1},{3,2},{4,3},{5,4},{6,5},{7,6},{0,7},{9,8},{10,9},{11,1... | collective-permute-start | bytes 393224 | tf_op jit(solution)/shard_map/ppermute | solution.py:23
  17.3 2.4 %scatter_custom_fusion = s32[512]{0:T(512)S(1)} fusion(s32[512]{0:T(512)S(1)} %bitcast.156, s32[512]{0:T(512)S(1)} %iota.61, s32[]{:T(128)} %copy.112), kind=kCustom, calls=%fused_computation.161 | custom fusion | bytes 2052 | tf_op jit(solution)/shard_map/scatter | solution.py:177
  22.0 1.9 %gather_fusion.6 = f32[256]{0:T(256)S(1)} fusion(f32[512]{0:T(512)S(1)} %get-tuple-element.139, s32[1024]{0:T(1024)S(1)} %pad_clamp_fusion.3), kind=kCustom, calls=%fused_computation.1.clone | custom fusion | bytes 3072 | tf_op jit(solution)/shard_map/jit(_take)/gather | solution.py:158
  24.0 1.9 %gather_fusion.7 = f32[256]{0:T(256)S(1)} fusion(f32[512]{0:T(512)S(1)} %get-tuple-element.140, s32[1024]{0:T(1024)S(1)} %pad_clamp_fusion.2), kind=kCustom, calls=%fused_computation.4.clone | custom fusion | bytes 3072 | tf_op jit(solution)/shard_map/jit(_take)/gather | solution.py:158
  26.0 1.8 %broadcast_select_fusion.1 = (f32[2,32,512]{1,0,2:T(2,128)S(1)}, f32[2,32,512]{1,0,2:T(2,128)S(1)}) fusion(f32[2,32,512]{1,0,2:T(2,128)S(1)} %collective-permute-done.4, pred[]{:T(512)S(6)} %lt.105, f32[512,2,32]{2,1,0:T(2,128)S(1)} %gather_fusion.2, pred[512]{0:T(512)(128)(4,1)S(1)} %get-tuple-element.99), kind=kLoop, calls=%fused_computation.96 | loop fusion | flops 98304 | bytes 524801 | tf_op jit(solution)/shard_map/jit(_where)/select_n | solution.py:146
  27.8 1.0 gather_fusion.4
  28.9 1.0 gather_fusion.5
  30.0 62.2 %while.10 = (s32[]{:T(128)}, f32[7,32,256]{2,1,0:T(8,128)S(1)}, f32[7,16]{1,0:T(8,128)S(1)}, f32[7,16,32]{2,1,0:T(8,128)S(1)}, f32[32,256]{1,0:T(8,128)S(1)}, /*...) while((s32[]{:T(128)}, f32[7,32,256]{2,1,0:T(8,128)S(1)}, f32[7,16]{1,0:T(8,128)S(1)}, ...), condition=%wide.region_3.6_spmd, body=%wide.region_0.5_spmd.sunk | while | flops 10227730 | bytes 32623476 | solution.py:86
  31.8 0.9 slice-done
  33.9 0.9 slice-done.1
  40.7 0.9 slice-done
  42.8 0.9 slice-done.1
  49.6 0.9 slice-done
  51.7 0.9 slice-done.1
  58.5 0.9 slice-done
  60.6 0.9 slice-done.1
  67.4 0.9 slice-done
  69.5 0.9 slice-done.1
  76.3 0.9 slice-done
  78.3 0.9 slice-done.1
  85.2 0.9 slice-done
  87.2 0.9 slice-done.1
  92.5 2.3 %collective-permute-start.2 = (f32[4,32,8,2]{3,1,2,0:T(8,128)S(1)}, f32[4,32,8,2]{3,1,2,0:T(8,128)S(1)}, u32[]{:S(2)}, u32[]{:S(2)}) collective-permute-start(f32[4,32,8,2]{3,1,2,0:T(8,128)S(1)} %get-tuple-element.127), channel_id=1, source_target_pairs={{0,8},{8,16},{16,24},{24,0},{1,9},{9,17},{17,25},{25,1},{2,10},{10... | collective-permute-start | bytes 24584 | tf_op jit(solution)/shard_map/ppermute | solution.py:20
  95.4 10.1 %collective-permute-done.2 = f32[4,32,8,2]{3,1,2,0:T(8,128)S(1)} collective-permute-done((f32[4,32,8,2]{3,1,2,0:T(8,128)S(1)}, f32[4,32,8,2]{3,1,2,0:T(8,128)S(1)}, u32[]{:S(2)}, u32[]{:S(2)}) %collective-permute-start.2) | collective-permute-done | bytes 8224 | tf_op jit(solution)/shard_map/ppermute | solution.py:20
  105.5 2.3 %collective-permute-done.3 = f32[4,32,8,2]{3,1,2,0:T(8,128)S(1)} collective-permute-done((f32[4,32,8,2]{3,1,2,0:T(8,128)S(1)}, f32[4,32,8,2]{3,1,2,0:T(8,128)S(1)}, u32[]{:S(2)}, u32[]{:S(2)}) %collective-permute-start.3) | collective-permute-done | bytes 8224 | tf_op jit(solution)/shard_map/ppermute | solution.py:23
  112.4 1.0 gather_fusion.8
  113.6 1.0 gather_fusion.9
  (612 shorter events, 57.4 us)
Async XLA Ops:
  1.4 3.5 %copy-start.10 = (s32[1,1,512]{2,1,0:T(1,128)S(1)}, s32[1,1,512]{2,1,0:T(1,128)}, u32[]{:S(2)}) copy-start(s32[1,1,512]{2,1,0:T(1,128)} %param.27) | copy-start | bytes 6148
  1.4 5.7 %copy-start.8 = (f32[32,4,128]{2,1,0:T(4,128)S(1)}, f32[32,4,128]{2,1,0:T(4,128)}, u32[]{:S(2)}) copy-start(f32[32,4,128]{2,1,0:T(4,128)} %param.18) | copy-start | bytes 196612
  4.9 2.2 %copy-start.7 = (f32[32,4,128]{2,1,0:T(4,128)S(1)}, f32[32,4,128]{2,1,0:T(4,128)}, u32[]{:S(2)}) copy-start(f32[32,4,128]{2,1,0:T(4,128)} %param.19) | copy-start | bytes 196612
  4.9 17.1 %collective-permute-start.5 = (f32[512]{0:T(512)S(1)}, f32[512]{0:T(512)S(1)}, u32[]{:S(2)}, u32[]{:S(2)}) collective-permute-start(f32[512]{0:T(512)S(1)} %get-tuple-element.98), channel_id=1, source_target_pairs={{0,16},{8,24},{16,0},{24,8},{1,17},{9,25},{17,1},{25,9},{2,18},{10... | collective-permute-start | bytes 6152 | tf_op jit(solution)/shard_map/ppermute | solution.py:11
  11.2 0.8 copy-start.5
  11.2 0.9 copy-start.6
  11.2 14.7 %collective-permute-start.4 = (f32[2,32,512]{1,0,2:T(2,128)S(1)}, f32[2,32,512]{1,0,2:T(2,128)S(1)}, u32[]{:S(2)}, u32[]{:S(2)}) collective-permute-start(f32[2,32,512]{1,0,2:T(2,128)S(1)} %select_bitcast_fusion), channel_id=1, source_target_pairs={{0,16},{8,24},{16,0},{24,8},{1,17},{9,25},{17,1},{25,9},{2,18},{10... | collective-permute-start | bytes 393224 | tf_op jit(solution)/shard_map/ppermute | solution.py:11
  12.2 80.1 %collective-permute-start = (f32[4,32,2,128]{3,1,2,0:T(8,128)S(1)}, f32[4,32,2,128]{3,1,2,0:T(8,128)S(1)}, u32[]{:S(2)}, u32[]{:S(2)}) collective-permute-start(f32[4,32,2,128]{3,1,2,0:T(8,128)S(1)} %get-tuple-element.129), channel_id=1, source_target_pairs={{0,1},{1,2},{2,3},{3,4},{4,5},{5,6},{6,7},{7,0},{8,9},{9,10},{10,1... | collective-permute-start | bytes 393224 | tf_op jit(solution)/shard_map/ppermute | solution.py:20
  13.4 78.9 %collective-permute-start.1 = (f32[4,32,2,128]{3,1,2,0:T(8,128)S(1)}, f32[4,32,2,128]{3,1,2,0:T(8,128)S(1)}, u32[]{:S(2)}, u32[]{:S(2)}) collective-permute-start(f32[4,32,2,128]{3,1,2,0:T(8,128)S(1)} %get-tuple-element.130), channel_id=1, source_target_pairs={{1,0},{2,1},{3,2},{4,3},{5,4},{6,5},{7,6},{0,7},{9,8},{10,9},{11,1... | collective-permute-start | bytes 393224 | tf_op jit(solution)/shard_map/ppermute | solution.py:23
  31.8 0.9 slice-start
  33.9 0.9 slice-start.1
  35.6 0.8 slice-start.2
  40.7 0.9 slice-start
  42.8 0.9 slice-start.1
  44.5 0.8 slice-start.2
  49.6 0.9 slice-start
  51.6 0.9 slice-start.1
  53.4 0.8 slice-start.2
  58.5 0.9 slice-start
  60.5 0.9 slice-start.1
  62.3 0.8 slice-start.2
  67.4 0.9 slice-start
  69.4 0.9 slice-start.1
  71.2 0.8 slice-start.2
  76.3 0.9 slice-start
  78.3 0.9 slice-start.1
  85.1 0.9 slice-start
  87.2 0.9 slice-start.1
  89.0 0.8 slice-start.2
  92.5 13.0 %collective-permute-start.2 = (f32[4,32,8,2]{3,1,2,0:T(8,128)S(1)}, f32[4,32,8,2]{3,1,2,0:T(8,128)S(1)}, u32[]{:S(2)}, u32[]{:S(2)}) collective-permute-start(f32[4,32,8,2]{3,1,2,0:T(8,128)S(1)} %get-tuple-element.127), channel_id=1, source_target_pairs={{0,8},{8,16},{16,24},{24,0},{1,9},{9,17},{17,25},{25,1},{2,10},{10... | collective-permute-start | bytes 24584 | tf_op jit(solution)/shard_map/ppermute | solution.py:20
  94.8 13.0 %collective-permute-start.3 = (f32[4,32,8,2]{3,1,2,0:T(8,128)S(1)}, f32[4,32,8,2]{3,1,2,0:T(8,128)S(1)}, u32[]{:S(2)}, u32[]{:S(2)}) collective-permute-start(f32[4,32,8,2]{3,1,2,0:T(8,128)S(1)} %get-tuple-element.128), channel_id=1, source_target_pairs={{8,0},{16,8},{24,16},{0,24},{9,1},{17,9},{25,17},{1,25},{10,2},{18... | collective-permute-start | bytes 24584 | tf_op jit(solution)/shard_map/ppermute | solution.py:23
  94.9 17.2 %collective-permute-start.6 = (f32[32,256]{1,0:T(8,128)S(1)}, f32[32,256]{1,0:T(8,128)S(1)}, u32[]{:S(2)}, u32[]{:S(2)}) collective-permute-start(f32[32,256]{1,0:T(8,128)S(1)} %broadcast_multiply_fusion.5), channel_id=1, source_target_pairs={{0,16},{8,24},{16,0},{24,8},{1,17},{9,25},{17,1},{25,9},{2,18},{10... | collective-permute-start | bytes 98312 | tf_op jit(solution)/shard_map/ppermute | solution.py:11
  (40 other events, 26.8 us)
where the time goes:
time: 117 us; the launch traced here: 116 us
  local copies, waits for them, and re-layouts  66.2 us (57%)
  other arithmetic  21.8 us (19%)
  waiting for transfers between devices  12.4 us (11%)
  starting transfers between devices  10.1 us (9%)
  loops' own time  3.11 us (3%)
  between operations  1.9 us (2%)
    while x56, local copies, waits for them, and re-layouts  18 us
    slice x49, local copies, waits for them, and re-layouts, cyclic(): next_rhs = jnp.concatenate([even_rhs[1:], edge_zero], axis=0)  16.6 us
    ppermute x2, waiting for transfers between devices, extended(): lax.ppermute(lax.slice_in_dim(block, block.shape[dim] - width, None, axis...  10.1 us
    slice x35, local copies, waits for them, and re-layouts, cyclic(): next_sub = jnp.concatenate([even_sub[1:], edge_zero], axis=0)  6.51 us
    unnamed x22, local copies, waits for them, and re-layouts  4.01 us
    add x28, other arithmetic, cyclic(): odd_rhs + alpha_term * even_rhs + gamma_term * next_rhs  3.72 us
    ppermute x2, starting transfers between devices, extended(): lax.ppermute(lax.slice_in_dim(block, block.shape[dim] - width, None, axis...  3.56 us
    gather x1, local copies, waits for them, and re-layouts, local(): own_cos = jnp.take(sun_height_ratio.reshape(profile_group), listing)  3.49 us
  transfers between devices with their start and end apart: 7, of which 2 were waited for; matrix products, arithmetic and copies ran while one was open for 32% of the time, Pallas kernels for 0%

commit v1 on v0

v1 whole, which is shorter than its diff:
```python
import math

import jax
import jax.numpy as jnp
import numpy as np
from jax import lax
from jax.experimental import pallas as pl
from jax.experimental.pallas import tpu as pltpu
from jax.sharding import PartitionSpec as P

heat_coeff = 20.0
f32, bf16 = jnp.float32, jnp.bfloat16
VMEM_SPEC = pl.BlockSpec(memory_space=pltpu.VMEM)
SMEM_SPEC = pl.BlockSpec(memory_space=pltpu.SMEM)
NT_DIMS = (((1,), (1,)), ((), ()))
TN_DIMS = (((0,), (0,)), ((), ()))


def iota(shape, dim):
    return lax.broadcasted_iota(jnp.int32, shape, dim)


def shape_of(*dims):
    return jax.ShapeDtypeStruct(dims, f32)


def swaps(count, first, ring):
    pairs = []
    for i in range(first, count, 2):
        j = i + 1
        if j == count and not ring:
            break
        pairs += [(i, j % count), (j % count, i)]
    return pairs


def rows_kernel(t, q, cx, cy, tally, perm, to_a, to_b, lit):
    total, lanes = t.shape
    rows = lit.shape[0]
    levels = total // rows
    even = lax.rem(lax.axis_index("lat"), 2) == 0

    def row(ref, r):
        return ref[pl.ds(r, levels, stride=rows), :]

    top = rows - 1
    picks = ((t, 0), (t, 1), (q, 0), (q, 1), (cx, 0), (cy, 0))
    for k, (ref, deep) in enumerate(picks):
        high, low = row(ref, top - deep), row(ref, deep)
        to_a[k * levels : (k + 1) * levels, :] = jnp.where(even, high, low)
        to_b[k * levels : (k + 1) * levels, :] = jnp.where(even, low, high)
    count = tally[0, 0]
    found = jnp.zeros((8, lanes), f32)
    for r in range(rows):
        column = perm[0, :, r * lanes : (r + 1) * lanes]
        row_at = column // lanes
        lane_at = column - row_at * lanes
        sunlit = iota((1, lanes), 1) + r * lanes < count
        at_row = jnp.where((row_at == iota((8, lanes), 0)) & sunlit, 1.0, 0.0).astype(bf16)
        at_lane = jnp.where(lane_at == iota((lanes, lanes), 0), 1.0, 0.0).astype(bf16)
        found += lax.dot_general(at_row, at_lane, NT_DIMS, preferred_element_type=f32)
    lit[...] = found[:rows]


def edge_rows(t, q, cx, cy, tally, perm, rows):
    total, lanes = t.shape
    levels = total // rows
    return pl.pallas_call(
        rows_kernel,
        out_shape=(shape_of(6 * levels, lanes), shape_of(6 * levels, lanes), shape_of(rows, lanes)),
        in_specs=[VMEM_SPEC] * 4 + [SMEM_SPEC, VMEM_SPEC],
        out_specs=(VMEM_SPEC,) * 3,
        name="edge_rows",
    )(t, q, cx, cy, tally, perm)


def columns_kernel(pad, t, q, cx, cy, from_a, from_b, ft, fq, fx, fy, own, to_a, to_b):
    total, lanes = t.shape
    levels = from_a.shape[0] // 6
    rows = total // levels
    tall = rows + 2 * pad
    lat = lax.axis_index("lat")
    even = lax.rem(lat, 2) == 0
    first, last = lat == 0, lat == lax.axis_size("lat") - 1
    outs = (ft, fq, fx, fy)
    refs = (t, q, cx, cy)
    slots = ((0, 1), (2, 3), (4,), (5,))
    for ref, out, at in zip(refs, outs, slots):
        inner = [ref[pl.ds(r, levels, stride=rows), :] for r in range(rows)]
        for r in range(rows):
            out[pl.ds(pad + r, levels, stride=tall), :] = inner[r]
        for deep in range(pad):
            k = at[min(deep, len(at) - 1)]
            a = from_a[k * levels : (k + 1) * levels, :]
            b = from_b[k * levels : (k + 1) * levels, :]
            south = jnp.where(first, inner[0], jnp.where(even, b, a))
            north = jnp.where(last, inner[rows - 1], jnp.where(even, a, b))
            out[pl.ds(pad - 1 - deep, levels, stride=tall), :] = south
            out[pl.ds(pad + rows + deep, levels, stride=tall), :] = north
    edges = jnp.zeros((16, levels * tall), f32)
    which = iota((16, lanes), 0)
    lane = iota((16, lanes), 1)
    for out, at in zip(outs, slots):
        pick = jnp.zeros((16, lanes), jnp.bool_)
        for deep, k in enumerate(at):
            pick |= (which == k) & (lane == lanes - 1 - deep)
            pick |= (which == 8 + k) & (lane == deep)
        edges += lax.dot_general(
            jnp.where(pick, 1.0, 0.0),
            out[...],
            NT_DIMS,
            precision=lax.Precision.HIGHEST,
            preferred_element_type=f32,
        )
    own[...] = edges
    even_lon = lax.rem(lax.axis_index("lon"), 2) == 0
    east, west = edges[:8], edges[8:]
    to_a[...] = jnp.where(even_lon, east, west)
    to_b[...] = jnp.where(even_lon, west, east)


def edge_columns(t, q, cx, cy, from_a, from_b, pad):
    import functools

    total, lanes = t.shape
    levels = from_a.shape[0] // 6
    tall = levels * (total // levels + 2 * pad)
    return pl.pallas_call(
        functools.partial(columns_kernel, pad),
        out_shape=(*[shape_of(tall, lanes)] * 4, shape_of(16, tall), shape_of(8, tall), shape_of(8, tall)),
        in_specs=[VMEM_SPEC] * 6,
        out_specs=(VMEM_SPEC,) * 7,
        name="edge_columns",
    )(t, q, cx, cy, from_a, from_b)


def weights(cx, cy):
    hx, hy = 0.5 * cx, 0.5 * cy
    sx, sy = hx * cx, hy * cy
    return 1.0 - 2.0 * (sx + sy), sx - hx, sx + hx, sy - hy, sy + hy


def blend(w, here, east, west, north, south):
    return w[0] * here + w[1] * east + w[2] * west + w[3] * north + w[4] * south


def advect_kernel(rows, pad, ft, fq, fx, fy, own, from_a, from_b, t_out, q_out, keep):
    tall, lanes = ft.shape
    high = rows + 2 * pad
    levels = tall // high
    even_lon = lax.rem(lax.axis_index("lon"), 2) == 0
    lat = lax.axis_index("lat")
    first, last = lat == 0, lat == lax.axis_size("lat") - 1
    a, b = from_a[...], from_b[...]
    east, west = jnp.where(even_lon, a, b), jnp.where(even_lon, b, a)
    mine = own[...]

    def strip(x, k):
        return x[k : k + 1, :]

    halo = []
    firsts = []
    ww = weights(strip(west, 4), strip(west, 5))
    we = weights(strip(east, 4), strip(east, 5))
    for k in (0, 2):
        near_w, near_e = strip(west, k), strip(east, k)
        halo += [near_w, near_e]
        up = lambda x: pltpu.roll(x, tall - 1, 1)
        down = lambda x: pltpu.roll(x, 1, 1)
        firsts.append(blend(ww, near_w, strip(mine, 8 + k), strip(west, k + 1), up(near_w), down(near_w)))
        firsts.append(blend(we, near_e, strip(east, k + 1), strip(mine, k), up(near_e), down(near_e)))
    stack = jnp.concatenate(halo + firsts, axis=0)
    source, target = iota((8, 4 * lanes), 0), iota((8, 4 * lanes), 1)
    wanted = (source // 2) * lanes + lax.rem(source, 2) * (lanes - 1)
    rims = lax.dot_general(
        stack,
        jnp.where(target == wanted, 1.0, 0.0),
        TN_DIMS,
        precision=lax.Precision.HIGHEST,
        preferred_element_type=f32,
    )
    cut = lambda x: x.reshape(levels, high, lanes)
    w = weights(cut(fx[...]), cut(fy[...]))
    full = (levels, high, lanes)
    lane, at = iota(full, 2), iota(full, 1)
    for k, (ref, out) in enumerate(((ft, t_out), (fq, q_out))):
        f = cut(ref[...])
        for step in range(2):
            rim = cut(rims[:, (2 * step + k) * lanes : (2 * step + k + 1) * lanes])
            e = jnp.where(lane == lanes - 1, rim, pltpu.roll(f, lanes - 1, 2))
            wst = jnp.where(lane == 0, rim, pltpu.roll(f, 1, 2))
            n = jnp.where(last & (at == pad + rows - 1), f, pltpu.roll(f, high - 1, 1))
            s = jnp.where(first & (at == pad), f, pltpu.roll(f, 1, 1))
            f = blend(w, f, e, wst, n, s)
        keep[...] = f.reshape(tall, lanes)
        for r in range(rows):
            out[pl.ds(r, levels, stride=rows), :] = keep[pl.ds(pad + r, levels, stride=high), :]


def advect(ft, fq, fx, fy, own, from_a, from_b, rows, pad):
    import functools

    tall, lanes = ft.shape
    total = tall // (rows + 2 * pad) * rows
    return pl.pallas_call(
        functools.partial(advect_kernel, rows, pad),
        out_shape=(shape_of(total, lanes), shape_of(total, lanes)),
        in_specs=[VMEM_SPEC] * 7,
        out_specs=(VMEM_SPEC,) * 2,
        scratch_shapes=[pltpu.VMEM((tall, lanes), f32)],
        name="advect",
    )(ft, fq, fx, fy, own, from_a, from_b)


def halves(x):
    high = x.astype(bf16)
    return high, (x - high.astype(f32)).astype(bf16)


def thirds(value):
    import ml_dtypes

    left, parts = np.float32(value), []
    for _ in range(3):
        part = np.float32(left.astype(ml_dtypes.bfloat16))
        parts.append(float(part))
        left = np.float32(left - part)
    return parts


SLOTS, AHEAD = 16, 8


def heating_kernel(
    t, q, mu, k, albedo, solar, lit, out,
    factor, linear, tables, masks, shares, albedos, trans, pull, beam, total,
):
    levels, gpoints = k.shape[1], k.shape[0]
    rows, lanes = mu.shape
    quarter = lanes // 4
    wide = 2 * lanes
    engines = rows // 2
    factor[...] = (1.5 + jnp.tanh(q[...])) * (1.0 + 0.25 * jnp.tanh(t[...]))
    ones = jnp.ones((quarter, lanes), bf16)
    for r in range(rows):
        level_factor = factor[pl.ds(r, levels, stride=rows), :]
        per_path = level_factor * (-math.log2(math.e) / mu[r : r + 1, :])
        for start, value in ((0, level_factor), (lanes, per_path)):
            high, low = halves(value)
            linear[start : start + lanes, r * lanes : (r + 1) * lanes] = jnp.concatenate(
                [high, high, low, ones], axis=0
            )
    square = iota((gpoints, gpoints), 0) == iota((gpoints, gpoints), 1)

    def upright(row):
        return jnp.sum(jnp.where(square, row, 0.0), axis=1, keepdims=True)

    w = upright(albedo[...])
    coeff = k[...]
    slot = iota((1, quarter), 1)

    def table(value, constants):
        high = value.astype(bf16).astype(f32)
        tail = jnp.zeros((1, quarter), f32)
        for i, c in enumerate(constants):
            tail = jnp.where(slot == i, c, tail)
        tail = jnp.broadcast_to(tail, (gpoints, quarter))
        return jnp.concatenate([high, value - high, high, tail], axis=1).astype(bf16)

    tables[0] = table(coeff, thirds(1.0 / 3.0))
    tables[1] = table(1.5 * (1.0 - w) * coeff, (0.75,))
    shares[...] = (1.0 - w) * upright(solar[...]) * coeff
    albedos[...] = jnp.broadcast_to(1.5 * w, (gpoints, lanes))
    lane = iota((16, lanes), 1)
    level, constant = lax.rem(lane, quarter), lane >= 3 * quarter
    for l in range(levels):
        masks[0, l] = jnp.where(constant | (level == l) | (level == l + 1), 1.0, 0.0).astype(bf16)
        masks[1, l] = jnp.where(constant | (level == l), 1.0, 0.0).astype(bf16)
        masks[2, l] = jnp.where(
            constant, 0.0, jnp.where(level < l, 1.0, jnp.where(level == l, 0.5, 0.0))
        ).astype(bf16)
    total[...] = jnp.zeros_like(total)
    units = [(a, b) for a in range(2) for b in range(rows)]
    each = range(len(units))

    def main(*sums):
        def at(m, l):
            return sums[m * SLOTS + l % SLOTS]

        def group(i):
            start = pl.multiple_of(i * 16, 16)
            starts = [pl.multiple_of(start + 8 * a, 8) for a in range(2)]
            plain, absorbing = (tables[j, pl.ds(start, 16), :] for j in range(2))
            w15 = [albedos[pl.ds(s, 8), :] for s in starts]
            share = [shares[pl.ds(s, 8), :] for s in starts]
            blank = jnp.zeros((16, lanes), bf16)

            def issue(l):
                stack = [
                    jnp.concatenate([plain * masks[0, l], blank], axis=1),
                    jnp.concatenate([absorbing * masks[1, l], blank], axis=1),
                    jnp.concatenate([blank, plain * masks[2, l]], axis=1),
                ]
                stack = jnp.concatenate(stack, axis=0)
                for m in range(engines):
                    pltpu.matmul_acc_lhs(at(m, l), stack)

            for l in range(AHEAD):
                issue(l)
            y = current = step = None
            for l in range(levels):
                if l + AHEAD < levels:
                    issue(l + AHEAD)
                popped = [pltpu.matmul_pop(at(m, l)) for m in range(engines)]

                def part(kind, a, b):
                    s = kind * 16 + a * 8
                    return popped[b // 2][s : s + 8, (b % 2) * lanes : (b % 2 + 1) * lanes]

                resist, shunt, path = ([part(i, a, b) for a, b in units] for i in range(3))
                direct = [jnp.exp2(p) for p in path]
                source = [w15[units[u][0]] * direct[u] for u in each]
                for u in each:
                    beam[u, l] = direct[u]
                if l == 0:
                    y, current = shunt, source
                else:
                    y = [shunt[u] + y[u] * step[u] for u in each]
                    current = [source[u] + current[u] * step[u] for u in each]
                if l < levels - 1:
                    step = [1.0 / (1.0 + resist[u] * y[u]) for u in each]
                    for u in each:
                        trans[u, l] = step[u]
                        pull[u, l] = resist[u] * current[u]
            diffuse = [current[u] / y[u] for u in each]
            for l in range(levels - 1, -1, -1):
                if l < levels - 1:
                    diffuse = [trans[u, l] * (pull[u, l] + diffuse[u]) for u in each]
                spread = [jnp.broadcast_to(share[a][:, l : l + 1], (8, lanes)) for a in range(2)]
                for b in range(rows):
                    pair = [
                        (diffuse[a * rows + b] + beam[a * rows + b, l]) * spread[a]
                        for a in range(2)
                    ]
                    total[l, b] = total[l, b] + (pair[0] + pair[1])

        nothing = jnp.zeros((16, wide), bf16)
        for m in range(engines):
            last = sums[engines * SLOTS + m]
            pltpu.matmul_push_rhs(linear[:, m * wide : (m + 1) * wide], 0, m)
            pltpu.matmul_acc_lhs(last, nothing, load_staged_rhs=0)
            pltpu.matmul_pop(last)
        pl.loop(0, gpoints // 16)(group)

    pl.run_scoped(
        main,
        *[pltpu.ACC(m)((48, wide), f32) for m in range(engines) for _ in range(SLOTS)],
        *[pltpu.ACC(m)((16, wide), f32) for m in range(engines)],
    )
    scale = heat_coeff * mu[...] * lit[...]
    for l in range(levels):
        here = pl.ds(l * rows, rows)
        out[here, :] = jnp.sum(total[l], axis=1) * scale * factor[here, :]


def heating(t, q, mu, k, albedo, solar, lit):
    rows, lanes = mu.shape
    gpoints, levels = k.shape
    units = 2 * rows
    stage = pltpu.VMEM((units, levels, 8, lanes), f32)
    return pl.pallas_call(
        heating_kernel,
        out_shape=shape_of(*t.shape),
        in_specs=[VMEM_SPEC] * 7,
        out_specs=VMEM_SPEC,
        scratch_shapes=[
            pltpu.VMEM(t.shape, f32),
            pltpu.VMEM((2 * lanes, rows * lanes), bf16),
            pltpu.VMEM((2, gpoints, lanes), bf16),
            pltpu.VMEM((3, levels, 16, lanes), bf16),
            pltpu.VMEM((gpoints, levels), f32),
            pltpu.VMEM((gpoints, lanes), f32),
            stage,
            stage,
            stage,
            pltpu.VMEM((levels, rows, 8, lanes), f32),
        ],
        cost_estimate=pl.CostEstimate(
            flops=40 * gpoints * levels * rows * lanes * 16, bytes_accessed=1 << 20, transcendentals=2 * gpoints * levels * rows * lanes
        ),
        name="heating",
    )(t, q, mu, k, albedo, solar, lit)


def local(
    thermal_deviation,
    moisture_deviation,
    eastward_stability,
    northward_stability,
    sun_height_ratio,
    extinction_coeff,
    reflectivity_ratio,
    insolation_source,
    daylight_tally,
    daylight_permutation,
):
    levels, rows, lanes = thermal_deviation.shape
    pad = 2
    lat_count, lon_count = lax.axis_size("lat"), lax.axis_size("lon")
    flat = lambda x: x.reshape(levels * rows, lanes)
    t, q, cx, cy = (
        flat(x)
        for x in (thermal_deviation, moisture_deviation, eastward_stability, northward_stability)
    )
    to_a, to_b, lit = edge_rows(t, q, cx, cy, daylight_tally, daylight_permutation, rows)
    lat_b = lax.ppermute(to_b, "lat", swaps(lat_count, 1, False))
    lat_a = lax.ppermute(to_a, "lat", swaps(lat_count, 0, False))
    warming = heating(
        t,
        q,
        sun_height_ratio,
        extinction_coeff,
        reflectivity_ratio.reshape(1, -1),
        insolation_source.reshape(1, -1),
        lit,
    )
    ft, fq, fx, fy, own, to_a, to_b = edge_columns(t, q, cx, cy, lat_a, lat_b, pad)
    lon_b = lax.ppermute(to_b, "lon", swaps(lon_count, 1, True))
    lon_a = lax.ppermute(to_a, "lon", swaps(lon_count, 0, True))
    t_next, q_next = advect(ft, fq, fx, fy, own, lon_a, lon_b, rows, pad)
    whole = lambda x: x.reshape(levels, rows, lanes)
    return whole(t_next), whole(q_next), whole(warming)


def solution(mesh):
    volume, surface = P(None, "lat", "lon"), P("lat", "lon")
    placed = (volume,) * 4 + (surface, P(), P(), P(), surface, P("lat", "lon", None))
    step = jax.shard_map(
        local, mesh=mesh, in_specs=placed, out_specs=(volume,) * 3, check_vma=False
    )
    return step
```

time: 117 us -> 27.7 us (0.24)
  the two profiles are of different devices: /device:TPU:1 before, /device:TPU:9 now
where the time goes in v1:
time: 27.7 us; the launch traced here: 27.4 us
  Pallas kernels  13.9 us (50%)
  starting transfers between devices  6.41 us (23%)
  waiting for transfers between devices  3.82 us (14%)
  local copies, waits for them, and re-layouts  1.95 us (7%)
  between operations  1.32 us (5%)
    pallas_call x1, Pallas kernels, heating(): pl.pallas_call(heating_kernel, out_shape=shape_of(*t.shape), in_specs=[VM...  7.27 us
    ppermute x1, waiting for transfers between devices, local(): lat_b = lax.ppermute(to_b, 'lat', swaps(lat_count, 1, False))  3.81 us
    pallas_call x1, Pallas kernels, advect(): pl.pallas_call(functools.partial(advect_kernel, rows, pad), out_shape=(sh...  2.68 us
    pallas_call x1, Pallas kernels, edge_columns(): pl.pallas_call(functools.partial(columns_kernel, pad), out_shape=(*[shape...  2.27 us
    ppermute x1, starting transfers between devices, local(): lon_a = lax.ppermute(to_a, 'lon', swaps(lon_count, 0, True))  2.1 us
    unnamed x11, local copies, waits for them, and re-layouts  1.95 us
    ppermute x1, starting transfers between devices, local(): lat_b = lax.ppermute(to_b, 'lat', swaps(lat_count, 1, False))  1.91 us
    pallas_call x1, Pallas kernels, edge_rows(): pl.pallas_call(rows_kernel, out_shape=(shape_of(6 * levels, lanes), shape...  1.71 us
  transfers between devices with their start and end apart: 4, of which 1 were waited for; matrix products, arithmetic and copies ran while one was open for 3% of the time, Pallas kernels for 27%

profile of v1, /device:TPU:9, one launch (start us, length us, event | category | flops | bytes accessed | tf_op | source)
XLA Modules:
  0.0 27.4 jit_solution(15759837349905681813)
XLA Ops:
  1.3 0.0 copy-start.2
  1.3 1.7 %edge_rows.1 = (f32[192,128]{1,0:T(8,128)}, f32[192,128]{1,0:T(8,128)}, f32[4,128]{1,0:T(4,128)}) custom-call(f32[128,128]{1,0:T(8,128)} %bitcast.13, f32[128,128]{1,0:T(8,128)} %bitcast.16, f32[128,128]{1,0:T(8,128)} %bitcast.9, f32[128,128]{1,0:T(8,128)} %bitcast.11, s32[1,1]{1,0:T(1,128)S(6)} %copy.14.tally, s32[1,1,512]{2,1,0:T(1,128)} %perm.1), custom_call_target="tpu_custom_call" | custom-call | tf_op jit(solution)/shard_map/edge_rows/pallas_call | solution.py:68
  3.0 1.2 %collective-permute-start = (f32[192,128]{1,0:T(8,128)}, f32[192,128]{1,0:T(8,128)S(1)}, u32[]{:S(2)}, u32[]{:S(2)}) collective-permute-start(f32[192,128]{1,0:T(8,128)} %get-tuple-element.15), channel_id=1, source_target_pairs={{0,1},{1,0},{2,3},{3,2},{4,5},{5,4},{6,7},{7,6},{8,9},{9,8},{10,11... | collective-permute-start | bytes 294920 | tf_op jit(solution)/shard_map/ppermute | solution.py:417
  4.2 1.9 %collective-permute-start.1 = (f32[192,128]{1,0:T(8,128)}, f32[192,128]{1,0:T(8,128)S(1)}, u32[]{:S(2)}, u32[]{:S(2)}) collective-permute-start(f32[192,128]{1,0:T(8,128)} %get-tuple-element.16), channel_id=1, source_target_pairs={{1,2},{2,1},{3,4},{4,3},{5,6},{6,5},{9,10},{10,9},{11,12},{12,11},... | collective-permute-start | bytes 294920 | tf_op jit(solution)/shard_map/ppermute | solution.py:416
  6.1 0.0 copy-done.2
  6.1 0.7 %copy.13.k = f32[112,32]{1,0:T(8,128)} copy(f32[112,32]{0,1:T(8,128)S(1)} %copy-done.2) | data formatting | bytes 28672 | tf_op args[5]
  6.9 0.0 collective-permute-done.from_a
  6.9 0.0 copy-start
  6.9 3.8 %collective-permute-done.1.from_b = f32[192,128]{1,0:T(8,128)S(1)} collective-permute-done((f32[192,128]{1,0:T(8,128)}, f32[192,128]{1,0:T(8,128)S(1)}, u32[]{:S(2)}, u32[]{:S(2)}) %collective-permute-start.1) | collective-permute-done | bytes 98336 | tf_op jit(solution)/shard_map/ppermute | solution.py:416
  10.7 0.0 copy-done
  10.7 0.0 copy-start.1
  10.7 0.6 %copy-done.1 = f32[192,128]{1,0:T(8,128)} copy-done((f32[192,128]{1,0:T(8,128)}, f32[192,128]{1,0:T(8,128)S(1)}, u32[]{:S(2)}) %copy-start.1) | copy-done | bytes 98328
  11.3 2.3 %edge_columns.1 = (f32[256,128]{1,0:T(8,128)}, f32[256,128]{1,0:T(8,128)}, f32[256,128]{1,0:T(8,128)}, f32[256,128]{1,0:T(8,128)}, f32[16,256]{1,0:T(8,128)}, /*index=5*/f32[8,256]{1,0:T(8,128)}, f32[8,256]{1,0:T(8,128)}) custom-call(f32[128,128]{1,0:T(8,128)} %bitcast.14, f32[128,128]{1,0:T(8,128)} %bitcast.17, f32[128,128]{1,0:T(8,128)} %bitcast.10, ...), custom_call_target="tpu_custom_call" | custom-call | tf_op jit(solution)/shard_map/edge_columns/pallas_call | solution.py:128
  13.6 2.1 %collective-permute-start.2 = (f32[8,256]{1,0:T(8,128)}, f32[8,256]{1,0:T(8,128)S(1)}, u32[]{:S(2)}, u32[]{:S(2)}) collective-permute-start(f32[8,256]{1,0:T(8,128)} %get-tuple-element.22), channel_id=1, source_target_pairs={{0,8},{8,0},{16,24},{24,16},{1,9},{9,1},{17,25},{25,17},{2,10},{10... | collective-permute-start | bytes 24584 | tf_op jit(solution)/shard_map/ppermute | solution.py:429
  15.7 1.2 %collective-permute-start.3 = (f32[8,256]{1,0:T(8,128)}, f32[8,256]{1,0:T(8,128)S(1)}, u32[]{:S(2)}, u32[]{:S(2)}) collective-permute-start(f32[8,256]{1,0:T(8,128)} %get-tuple-element.23), channel_id=1, source_target_pairs={{8,16},{16,8},{24,0},{0,24},{9,17},{17,9},{25,1},{1,25},{10,18},{1... | collective-permute-start | bytes 24584 | tf_op jit(solution)/shard_map/ppermute | solution.py:428
  16.9 7.3 %heating.1 = f32[128,128]{1,0:T(8,128)} custom-call(f32[128,128]{1,0:T(8,128)} %bitcast.15, f32[128,128]{1,0:T(8,128)} %bitcast.18, f32[4,128]{1,0:T(4,128)} %mu.1, f32[112,32]{1,0:T(8,128)} %copy.13.k, f32[1,112]{1,0:T(1,128)} %bitcast.21, f32[1,112]{1,0:T(1,128)} %bitcast.22, f32[4,128]{1,0:T(4,128)} %get-tuple-element.26.lit), custom_call_target="tpu_custom_call" | custom-call | flops 1174405120 | bytes 1048576 | tf_op jit(solution)/shard_map/heating/pallas_call | solution.py:371
  24.1 0.0 collective-permute-done.2.from_a
  24.2 0.0 copy-start.3
  24.2 0.0 collective-permute-done.3.from_b
  24.2 0.0 copy-start.4
  24.2 0.6 %copy-done.3 = f32[8,256]{1,0:T(8,128)} copy-done((f32[8,256]{1,0:T(8,128)}, f32[8,256]{1,0:T(8,128)S(1)}, u32[]{:S(2)}) %copy-start.3) | copy-done | bytes 8216
  24.7 0.0 copy-done.4
  24.8 2.7 %advect.1 = (f32[128,128]{1,0:T(8,128)}, f32[128,128]{1,0:T(8,128)}) custom-call(f32[256,128]{1,0:T(8,128)} %get-tuple-element.17.ft, f32[256,128]{1,0:T(8,128)} %get-tuple-element.18.fq, f32[256,128]{1,0:T(8,128)} %get-tuple-element.19.fx, f32[256,128]{1,0:T(8,128)} %get-tuple-element.20.fy, f32[16,256]{1,0:T(8,128)} %get-tuple-element.21.own, ...), custom_call_target="tpu_custom_call" | custom-call | tf_op jit(solution)/shard_map/advect/pallas_call | solution.py:205
Async XLA Ops:
  1.3 4.9 %copy-start.2 = (f32[112,32]{0,1:T(8,128)S(1)}, f32[112,32]{0,1:T(8,128)}, u32[]{:S(2)}) copy-start(f32[112,32]{0,1:T(8,128)} %param.15) | copy-start | bytes 43012
  3.0 3.9 %collective-permute-start = (f32[192,128]{1,0:T(8,128)}, f32[192,128]{1,0:T(8,128)S(1)}, u32[]{:S(2)}, u32[]{:S(2)}) collective-permute-start(f32[192,128]{1,0:T(8,128)} %get-tuple-element.15), channel_id=1, source_target_pairs={{0,1},{1,0},{2,3},{3,2},{4,5},{5,4},{6,7},{7,6},{8,9},{9,8},{10,11... | collective-permute-start | bytes 294920 | tf_op jit(solution)/shard_map/ppermute | solution.py:417
  4.2 6.5 %collective-permute-start.1 = (f32[192,128]{1,0:T(8,128)}, f32[192,128]{1,0:T(8,128)S(1)}, u32[]{:S(2)}, u32[]{:S(2)}) collective-permute-start(f32[192,128]{1,0:T(8,128)} %get-tuple-element.16), channel_id=1, source_target_pairs={{1,2},{2,1},{3,4},{4,3},{5,6},{6,5},{9,10},{10,9},{11,12},{12,11},... | collective-permute-start | bytes 294920 | tf_op jit(solution)/shard_map/ppermute | solution.py:416
  6.9 3.8 %copy-start = (f32[192,128]{1,0:T(8,128)}, f32[192,128]{1,0:T(8,128)S(1)}, u32[]{:S(2)}) copy-start(f32[192,128]{1,0:T(8,128)S(1)} %collective-permute-done.from_a) | copy-start | bytes 294916
  10.7 0.6 %copy-start.1 = (f32[192,128]{1,0:T(8,128)}, f32[192,128]{1,0:T(8,128)S(1)}, u32[]{:S(2)}) copy-start(f32[192,128]{1,0:T(8,128)S(1)} %collective-permute-done.1.from_b) | copy-start | bytes 294916
  13.6 10.6 %collective-permute-start.2 = (f32[8,256]{1,0:T(8,128)}, f32[8,256]{1,0:T(8,128)S(1)}, u32[]{:S(2)}, u32[]{:S(2)}) collective-permute-start(f32[8,256]{1,0:T(8,128)} %get-tuple-element.22), channel_id=1, source_target_pairs={{0,8},{8,0},{16,24},{24,16},{1,9},{9,1},{17,25},{25,17},{2,10},{10... | collective-permute-start | bytes 24584 | tf_op jit(solution)/shard_map/ppermute | solution.py:429
  15.7 8.5 %collective-permute-start.3 = (f32[8,256]{1,0:T(8,128)}, f32[8,256]{1,0:T(8,128)S(1)}, u32[]{:S(2)}, u32[]{:S(2)}) collective-permute-start(f32[8,256]{1,0:T(8,128)} %get-tuple-element.23), channel_id=1, source_target_pairs={{8,16},{16,8},{24,0},{0,24},{9,17},{17,9},{25,1},{1,25},{10,18},{1... | collective-permute-start | bytes 24584 | tf_op jit(solution)/shard_map/ppermute | solution.py:428
  24.2 0.6 %copy-start.3 = (f32[8,256]{1,0:T(8,128)}, f32[8,256]{1,0:T(8,128)S(1)}, u32[]{:S(2)}) copy-start(f32[8,256]{1,0:T(8,128)S(1)} %collective-permute-done.2.from_a) | copy-start | bytes 24580
  24.2 0.6 %copy-start.4 = (f32[8,256]{1,0:T(8,128)}, f32[8,256]{1,0:T(8,128)S(1)}, u32[]{:S(2)}) copy-start(f32[8,256]{1,0:T(8,128)S(1)} %collective-permute-done.3.from_b) | copy-start | bytes 24580

commit v2 on v1

v2 whole, which is shorter than its diff:
```python
import functools
import math

import jax
import jax.numpy as jnp
import ml_dtypes
import numpy as np
from jax import lax
from jax.experimental import pallas as pl
from jax.experimental.pallas import tpu as pltpu
from jax.sharding import PartitionSpec as P

heat_coeff = 20.0
f32, bf16 = jnp.float32, jnp.bfloat16
HELD = pltpu.VMEM
VMEM_SPEC = pl.BlockSpec(memory_space=pltpu.VMEM)
SMEM_SPEC = pl.BlockSpec(memory_space=pltpu.SMEM)
NT_DIMS = (((1,), (1,)), ((), ()))
TN_DIMS = (((0,), (0,)), ((), ()))


def iota(shape, dim):
    return lax.broadcasted_iota(jnp.int32, shape, dim)


def shape_of(*dims):
    return jax.ShapeDtypeStruct(dims, f32)


def held(*arrays):
    return [pltpu.with_memory_space_constraint(x, pltpu.VMEM) for x in arrays]


def swaps(count, first, ring):
    pairs = []
    for i in range(first, count, 2):
        j = i + 1
        if j == count and not ring:
            break
        pairs += [(i, j % count), (j % count, i)]
    return pairs


def rows_kernel(rows, t, q, cx, cy, to_a, to_b):
    levels = t.shape[0] // rows
    even = lax.rem(lax.axis_index("lat"), 2) == 0

    def row(ref, r):
        return ref[pl.ds(r, levels, stride=rows), :]

    picks = ((t, 0), (t, 1), (q, 0), (q, 1), (cx, 0), (cy, 0))
    for k, (ref, deep) in enumerate(picks):
        high, low = row(ref, rows - 1 - deep), row(ref, deep)
        to_a[k * levels : (k + 1) * levels, :] = jnp.where(even, high, low)
        to_b[k * levels : (k + 1) * levels, :] = jnp.where(even, low, high)


def edge_rows(t, q, cx, cy, rows):
    total, lanes = t.shape
    shape = (6 * (total // rows), lanes)
    return pl.pallas_call(
        functools.partial(rows_kernel, rows),
        out_shape=(HELD(shape, f32),) * 2,
        in_specs=[VMEM_SPEC] * 4,
        out_specs=(VMEM_SPEC,) * 2,
        name="edge_rows",
    )(t, q, cx, cy)


def halves(x):
    high = x.astype(bf16)
    return high, (x - high.astype(f32)).astype(bf16)


def thirds(value):
    left, parts = np.float32(value), []
    for _ in range(3):
        part = np.float32(left.astype(ml_dtypes.bfloat16))
        parts.append(float(part))
        left = np.float32(left - part)
    return parts


def pick_edges(slots, lanes, blocks):
    which, lane = iota((16, lanes), 0), iota((16, lanes), 1)
    edges = None
    for block, at in zip(blocks, slots):
        pick = jnp.zeros((16, lanes), jnp.bool_)
        for deep, k in enumerate(at):
            pick |= (which == k) & (lane == lanes - 1 - deep)
            pick |= (which == 8 + k) & (lane == deep)
        part = lax.dot_general(
            jnp.where(pick, 1.0, 0.0),
            block,
            NT_DIMS,
            precision=lax.Precision.HIGHEST,
            preferred_element_type=f32,
        )
        edges = part if edges is None else edges + part
    return edges


def prepare_kernel(
    pad, t, q, cx, cy, mu, k, albedo, solar, tally, perm,
    factor, linear, tables, masks, shares, albedos, scale, ft, fq, fx, fy, own,
):
    levels, gpoints = k.shape
    rows, lanes = mu.shape
    tall = rows + 2 * pad
    blocks = (t, q, cx, cy)
    for ref, out in zip(blocks, (ft, fq, fx, fy)):
        for r in range(rows):
            out[pl.ds(pad + r, levels, stride=tall), :] = ref[pl.ds(r, levels, stride=rows), :]
    own[...] = pick_edges(((0, 1), (2, 3), (4,), (5,)), lanes, [ref[...] for ref in blocks])

    count = tally[0, 0]
    found = jnp.zeros((8, lanes), f32)
    for r in range(rows):
        column = perm[0, :, r * lanes : (r + 1) * lanes]
        row_at = column // lanes
        lane_at = column - row_at * lanes
        sunlit = iota((1, lanes), 1) + r * lanes < count
        at_row = jnp.where((row_at == iota((8, lanes), 0)) & sunlit, 1.0, 0.0).astype(bf16)
        at_lane = jnp.where(lane_at == iota((lanes, lanes), 0), 1.0, 0.0).astype(bf16)
        found += lax.dot_general(at_row, at_lane, NT_DIMS, preferred_element_type=f32)
    scale[...] = heat_coeff * mu[...] * found[:rows]

    quarter = lanes // 4
    factor[...] = (1.5 + jnp.tanh(q[...])) * (1.0 + 0.25 * jnp.tanh(t[...]))
    ones = jnp.ones((quarter, lanes), bf16)
    for r in range(rows):
        level_factor = factor[pl.ds(r, levels, stride=rows), :]
        per_path = level_factor * (-math.log2(math.e) / mu[r : r + 1, :])
        for start, value in ((0, level_factor), (lanes, per_path)):
            high, low = halves(value)
            linear[start : start + lanes, r * lanes : (r + 1) * lanes] = jnp.concatenate(
                [high, high, low, ones], axis=0
            )
    square = iota((gpoints, gpoints), 0) == iota((gpoints, gpoints), 1)

    def upright(row):
        return jnp.sum(jnp.where(square, row, 0.0), axis=1, keepdims=True)

    w = upright(albedo[...])
    filled = jnp.concatenate([k[...], jnp.zeros((levels, lanes - gpoints), f32)], axis=1)
    coeff = jnp.transpose(filled)[:gpoints]
    slot = iota((1, quarter), 1)

    def table(value, constants):
        high = value.astype(bf16).astype(f32)
        tail = jnp.zeros((1, quarter), f32)
        for i, c in enumerate(constants):
            tail = jnp.where(slot == i, c, tail)
        tail = jnp.broadcast_to(tail, (gpoints, quarter))
        return jnp.concatenate([high, value - high, high, tail], axis=1).astype(bf16)

    tables[0] = table(coeff, thirds(1.0 / 3.0))
    tables[1] = table(1.5 * (1.0 - w) * coeff, (0.75,))
    shares[...] = (1.0 - w) * upright(solar[...]) * coeff
    albedos[...] = jnp.broadcast_to(1.5 * w, (gpoints, lanes))
    lane = iota((16, lanes), 1)
    level, constant = lax.rem(lane, quarter), lane >= 3 * quarter
    for l in range(levels):
        masks[0, l] = jnp.where(constant | (level == l) | (level == l + 1), 1.0, 0.0).astype(bf16)
        masks[1, l] = jnp.where(constant | (level == l), 1.0, 0.0).astype(bf16)
        masks[2, l] = jnp.where(
            constant, 0.0, jnp.where(level < l, 1.0, jnp.where(level == l, 0.5, 0.0))
        ).astype(bf16)


def prepare(t, q, cx, cy, mu, k, albedo, solar, tally, perm, pad):
    levels, gpoints = k.shape
    rows, lanes = mu.shape
    tall = levels * (rows + 2 * pad)
    return pl.pallas_call(
        functools.partial(prepare_kernel, pad),
        out_shape=(
            HELD(t.shape, f32),
            HELD((2 * lanes, rows * lanes), bf16),
            HELD((2, gpoints, lanes), bf16),
            HELD((3, levels, 16, lanes), bf16),
            HELD((gpoints, levels), f32),
            HELD((gpoints, lanes), f32),
            HELD((rows, lanes), f32),
            *[HELD((tall, lanes), f32)] * 4,
            HELD((16, levels * rows), f32),
        ),
        in_specs=[VMEM_SPEC] * 8 + [SMEM_SPEC, VMEM_SPEC],
        out_specs=(VMEM_SPEC,) * 12,
        cost_estimate=pl.CostEstimate(flops=1 << 22, bytes_accessed=1 << 21, transcendentals=1 << 17),
        name="prepare",
    )(t, q, cx, cy, mu, k, albedo, solar, tally, perm)


def by_side(even, first, last, from_a, from_b, k, levels, low, high):
    a, b = from_a[k * levels : (k + 1) * levels, :], from_b[k * levels : (k + 1) * levels, :]
    south, north = jnp.where(even, b, a), jnp.where(even, a, b)
    return jnp.where(first, low, south), jnp.where(last, high, north)


def lat_place():
    lat = lax.axis_index("lat")
    return lax.rem(lat, 2) == 0, lat == 0, lat == lax.axis_size("lat") - 1


def columns_kernel(pad, ft, fq, own, from_a, from_b, edges, to_a, to_b, ring):
    levels = from_a.shape[0] // 6
    total, lanes = ring.shape[1:]
    rows = total // levels
    tall = rows + 2 * pad
    ring[...] = jnp.zeros_like(ring)
    for i, ref in enumerate((ft, fq)):
        low, high = (ref[pl.ds(pad + r, levels, stride=tall), :] for r in (0, rows - 1))
        south, north = by_side(*lat_place(), from_a, from_b, 2 * i, levels, low, high)
        ring[i, pl.ds(0, levels, stride=rows), :] = south
        ring[i, pl.ds(rows - 1, levels, stride=rows), :] = north
    both = own[...] + pick_edges(((6,), (7,)), lanes, [ring[0], ring[1]])
    edges[...] = both
    even_lon = lax.rem(lax.axis_index("lon"), 2) == 0
    east, west = both[:8], both[8:]
    to_a[...] = jnp.where(even_lon, east, west)
    to_b[...] = jnp.where(even_lon, west, east)


def edge_columns(ft, fq, own, from_a, from_b, rows, pad):
    lanes = ft.shape[1]
    total = own.shape[1]
    return pl.pallas_call(
        functools.partial(columns_kernel, pad),
        out_shape=(HELD((16, total), f32), HELD((8, total), f32), HELD((8, total), f32)),
        in_specs=[VMEM_SPEC] * 5,
        out_specs=(VMEM_SPEC,) * 3,
        scratch_shapes=[pltpu.VMEM((2, total, lanes), f32)],
        name="edge_columns",
    )(*held(ft, fq, own, from_a, from_b))


def weights(cx, cy):
    hx, hy = 0.5 * cx, 0.5 * cy
    sx, sy = hx * cx, hy * cy
    return 1.0 - 2.0 * (sx + sy), sx - hx, sx + hx, sy - hy, sy + hy


def blend(w, here, east, west, north, south):
    return w[0] * here + w[1] * east + w[2] * west + w[3] * north + w[4] * south


def advect_kernel(
    rows, pad, ft, fq, fx, fy, edges, lat_a, lat_b, lon_a, lon_b, t_out, q_out, gt, gq, gx, gy, st, sq
):
    lanes = ft.shape[1]
    high = rows + 2 * pad
    levels = ft.shape[0] // high
    total = levels * rows
    place = lat_place()
    _, first, last = place
    grids = (gt, gq, gx, gy)
    for ref, grid, at in zip((ft, fq, fx, fy), grids, ((0, 1), (2, 3), (4,), (5,))):
        grid[...] = ref[...]
        low, top = (ref[pl.ds(pad + r, levels, stride=high), :] for r in (0, rows - 1))
        for deep in range(pad):
            k = at[min(deep, len(at) - 1)]
            south, north = by_side(*place, lat_a, lat_b, k, levels, low, top)
            grid[pl.ds(pad - 1 - deep, levels, stride=high), :] = south
            grid[pl.ds(pad + rows + deep, levels, stride=high), :] = north
    even_lon = lax.rem(lax.axis_index("lon"), 2) == 0
    a, b = lon_a[...], lon_b[...]
    east, west = jnp.where(even_lon, a, b), jnp.where(even_lon, b, a)
    mine = edges[...]

    def strip(x, k):
        return x[k : k + 1, :]

    row_of = lax.rem(iota((1, total), 1), rows)

    def up(x, k):
        return jnp.where(row_of == rows - 1, strip(x, 6 + k // 2), pltpu.roll(strip(x, k), total - 1, 1))

    def down(x, k):
        return jnp.where(row_of == 0, strip(x, 6 + k // 2), pltpu.roll(strip(x, k), 1, 1))

    ww = weights(strip(west, 4), strip(west, 5))
    we = weights(strip(east, 4), strip(east, 5))
    firsts = []
    for k in (0, 2):
        firsts.append(blend(ww, strip(west, k), strip(mine, 8 + k), strip(west, k + 1), up(west, k), down(west, k)))
        firsts.append(blend(we, strip(east, k), strip(east, k + 1), strip(mine, k), up(east, k), down(east, k)))
    stack = jnp.concatenate(
        [strip(x, k) for k in (0, 2, 6, 7) for x in (west, east)] + firsts + [jnp.zeros((4, total), f32)],
        axis=0,
    )
    source, target = iota((16, 6 * lanes), 0), iota((16, 6 * lanes), 1)
    wanted = (source // 2) * lanes + lax.rem(source, 2) * (lanes - 1)
    rims = lax.dot_general(
        stack,
        jnp.where((target == wanted) & (source < 12), 1.0, 0.0),
        TN_DIMS,
        precision=lax.Precision.HIGHEST,
        preferred_element_type=f32,
    )
    spread = (st, sq)
    cut = lambda x: x.reshape(levels, high, lanes)
    flat = lambda i: rims[:, i * lanes : (i + 1) * lanes]
    w = weights(cut(gx[...]), cut(gy[...]))
    full = (levels, high, lanes)
    lane, at = iota(full, 2), iota(full, 1)
    for k, (ref, out, rim_ref) in enumerate(((gt, t_out, st), (gq, q_out, sq))):
        f = cut(ref[...])
        for step in range(2):
            rim_ref[step, 0] = flat((0, 4)[step] + k)
            if step == 0:
                rim_ref[step, 1] = flat(2 + k)
            tall_rim = ref
            for r in range(rows):
                tall_rim[pl.ds(pad + r, levels, stride=high), :] = rim_ref[step, 0, pl.ds(r, levels, stride=rows), :]
            if step == 0:
                tall_rim[pl.ds(pad - 1, levels, stride=high), :] = rim_ref[step, 1, pl.ds(0, levels, stride=rows), :]
                tall_rim[pl.ds(pad + rows, levels, stride=high), :] = rim_ref[
                    step, 1, pl.ds(rows - 1, levels, stride=rows), :
                ]
            rim = cut(tall_rim[...])
            e = jnp.where(lane == lanes - 1, rim, pltpu.roll(f, lanes - 1, 2))
            wst = jnp.where(lane == 0, rim, pltpu.roll(f, 1, 2))
            n = jnp.where(last & (at == pad + rows - 1), f, pltpu.roll(f, high - 1, 1))
            s = jnp.where(first & (at == pad), f, pltpu.roll(f, 1, 1))
            f = blend(w, f, e, wst, n, s)
        ref[...] = f.reshape(levels * high, lanes)
        for r in range(rows):
            out[pl.ds(r, levels, stride=rows), :] = ref[pl.ds(pad + r, levels, stride=high), :]


def advect(ft, fq, fx, fy, edges, lat_a, lat_b, lon_a, lon_b, rows, pad):
    tall, lanes = ft.shape
    total = edges.shape[1]
    grid = pltpu.VMEM((tall, lanes), f32)
    return pl.pallas_call(
        functools.partial(advect_kernel, rows, pad),
        out_shape=(shape_of(total, lanes), shape_of(total, lanes)),
        in_specs=[VMEM_SPEC] * 9,
        out_specs=(VMEM_SPEC,) * 2,
        scratch_shapes=[grid] * 4 + [pltpu.VMEM((2, 2, total, lanes), f32)] * 2,
        name="advect",
    )(*held(ft, fq, fx, fy, edges, lat_a, lat_b, lon_a, lon_b))

SLOTS, AHEAD = 16, 8


def heating_kernel(
    factor, linear, tables, masks, shares, albedos, scale, out, trans, pull, beam, total
):
    gpoints, levels = shares.shape
    rows, lanes = scale.shape
    wide = 2 * lanes
    engines = rows // 2
    total[...] = jnp.zeros_like(total)
    units = [(a, b) for a in range(2) for b in range(rows)]
    each = range(len(units))

    def main(*sums):
        def at(m, l):
            return sums[m * SLOTS + l % SLOTS]

        def group(i):
            start = pl.multiple_of(i * 16, 16)
            starts = [pl.multiple_of(start + 8 * a, 8) for a in range(2)]
            plain, absorbing = (tables[j, pl.ds(start, 16), :] for j in range(2))
            w15 = [albedos[pl.ds(s, 8), :] for s in starts]
            share = [shares[pl.ds(s, 8), :] for s in starts]
            blank = jnp.zeros((16, lanes), bf16)

            def issue(l):
                stack = [
                    jnp.concatenate([plain * masks[0, l], blank], axis=1),
                    jnp.concatenate([absorbing * masks[1, l], blank], axis=1),
                    jnp.concatenate([blank, plain * masks[2, l]], axis=1),
                ]
                stack = jnp.concatenate(stack, axis=0)
                for m in range(engines):
                    pltpu.matmul_acc_lhs(at(m, l), stack)

            for l in range(AHEAD):
                issue(l)
            y = current = step = None
            for l in range(levels):
                if l + AHEAD < levels:
                    issue(l + AHEAD)
                popped = [pltpu.matmul_pop(at(m, l)) for m in range(engines)]

                def part(kind, a, b):
                    s = kind * 16 + a * 8
                    return popped[b // 2][s : s + 8, (b % 2) * lanes : (b % 2 + 1) * lanes]

                resist, shunt, path = ([part(i, a, b) for a, b in units] for i in range(3))
                direct = [jnp.exp2(p) for p in path]
                source = [w15[units[u][0]] * direct[u] for u in each]
                for u in each:
                    beam[u, l] = direct[u]
                if l == 0:
                    y, current = shunt, source
                else:
                    y = [shunt[u] + y[u] * step[u] for u in each]
                    current = [source[u] + current[u] * step[u] for u in each]
                if l < levels - 1:
                    step = [1.0 / (1.0 + resist[u] * y[u]) for u in each]
                    for u in each:
                        trans[u, l] = step[u]
                        pull[u, l] = resist[u] * current[u]
            diffuse = [current[u] / y[u] for u in each]
            for l in range(levels - 1, -1, -1):
                if l < levels - 1:
                    diffuse = [trans[u, l] * (pull[u, l] + diffuse[u]) for u in each]
                spread = [jnp.broadcast_to(share[a][:, l : l + 1], (8, lanes)) for a in range(2)]
                for b in range(rows):
                    pair = [
                        (diffuse[a * rows + b] + beam[a * rows + b, l]) * spread[a]
                        for a in range(2)
                    ]
                    total[l, b] = total[l, b] + (pair[0] + pair[1])

        nothing = jnp.zeros((16, wide), bf16)
        for m in range(engines):
            last = sums[engines * SLOTS + m]
            pltpu.matmul_push_rhs(linear[:, m * wide : (m + 1) * wide], 0, m)
            pltpu.matmul_acc_lhs(last, nothing, load_staged_rhs=0)
            pltpu.matmul_pop(last)
        pl.loop(0, gpoints // 16)(group)

    pl.run_scoped(
        main,
        *[pltpu.ACC(m)((48, wide), f32) for m in range(engines) for _ in range(SLOTS)],
        *[pltpu.ACC(m)((16, wide), f32) for m in range(engines)],
    )
    column_scale = scale[...]
    for l in range(levels):
        here = pl.ds(l * rows, rows)
        out[here, :] = jnp.sum(total[l], axis=1) * column_scale * factor[here, :]


def heating(factor, linear, tables, masks, shares, albedos, scale):
    rows, lanes = scale.shape
    gpoints, levels = shares.shape
    stage = pltpu.VMEM((2 * rows, levels, 8, lanes), f32)
    cells = gpoints * levels * rows * lanes
    return pl.pallas_call(
        heating_kernel,
        out_shape=shape_of(levels * rows, lanes),
        in_specs=[VMEM_SPEC] * 7,
        out_specs=VMEM_SPEC,
        scratch_shapes=[stage, stage, stage, pltpu.VMEM((levels, rows, 8, lanes), f32)],
        cost_estimate=pl.CostEstimate(flops=640 * cells, bytes_accessed=1 << 20, transcendentals=2 * cells),
        name="heating",
    )(*held(factor, linear, tables, masks, shares, albedos, scale))

def local(
    thermal_deviation,
    moisture_deviation,
    eastward_stability,
    northward_stability,
    sun_height_ratio,
    extinction_coeff,
    reflectivity_ratio,
    insolation_source,
    daylight_tally,
    daylight_permutation,
):
    levels, rows, lanes = thermal_deviation.shape
    pad = 2
    lat_count, lon_count = lax.axis_size("lat"), lax.axis_size("lon")
    flat = lambda x: x.reshape(levels * rows, lanes)
    t, q, cx, cy = (
        flat(x)
        for x in (thermal_deviation, moisture_deviation, eastward_stability, northward_stability)
    )
    to_a, to_b = edge_rows(t, q, cx, cy, rows)
    lat_b = lax.ppermute(to_b, "lat", swaps(lat_count, 1, False))
    lat_a = lax.ppermute(to_a, "lat", swaps(lat_count, 0, False))
    *tables, ft, fq, fx, fy, own = prepare(
        t,
        q,
        cx,
        cy,
        sun_height_ratio,
        jnp.transpose(extinction_coeff),
        reflectivity_ratio.reshape(1, -1),
        insolation_source.reshape(1, -1),
        daylight_tally,
        daylight_permutation,
        pad,
    )
    edges, to_a, to_b = edge_columns(ft, fq, own, lat_a, lat_b, rows, pad)
    lon_b = lax.ppermute(to_b, "lon", swaps(lon_count, 1, True))
    lon_a = lax.ppermute(to_a, "lon", swaps(lon_count, 0, True))
    warming = heating(*tables)
    t_next, q_next = advect(ft, fq, fx, fy, edges, lat_a, lat_b, lon_a, lon_b, rows, pad)
    whole = lambda x: x.reshape(levels, rows, lanes)
    return whole(t_next), whole(q_next), whole(warming)


def solution(mesh):
    volume, surface = P(None, "lat", "lon"), P("lat", "lon")
    placed = (volume,) * 4 + (surface, P(), P(), P(), surface, P("lat", "lon", None))
    step = jax.shard_map(
        local, mesh=mesh, in_specs=placed, out_specs=(volume,) * 3, check_vma=False
    )
    return step
```

time: 27.7 us -> 20.8 us (0.75)
  the two profiles are of different devices: /device:TPU:9 before, /device:TPU:17 now
where the time goes in v2:
time: 20.8 us; the launch traced here: 20.6 us
  Pallas kernels  10.9 us (52%)
  starting transfers between devices  6.6 us (32%)
  waiting for transfers between devices  1.84 us (9%)
  between operations  1.3 us (6%)
    pallas_call x1, Pallas kernels, heating(): pl.pallas_call(heating_kernel, out_shape=shape_of(levels * rows, lanes),...  6.23 us
    ppermute x1, starting transfers between devices, local(): lon_a = lax.ppermute(to_a, 'lon', swaps(lon_count, 0, True))  2.13 us
    ppermute x1, starting transfers between devices, local(): lat_b = lax.ppermute(to_b, 'lat', swaps(lat_count, 1, False))  2.04 us
    ppermute x1, waiting for transfers between devices, local(): lat_b = lax.ppermute(to_b, 'lat', swaps(lat_count, 1, False))  1.82 us
    pallas_call x1, Pallas kernels, prepare(): pl.pallas_call(functools.partial(prepare_kernel, pad), out_shape=(HELD(t....  1.72 us
    pallas_call x1, Pallas kernels, advect(): pl.pallas_call(functools.partial(advect_kernel, rows, pad), out_shape=(sh...  1.62 us
    ppermute x1, starting transfers between devices, local(): lat_a = lax.ppermute(to_a, 'lat', swaps(lat_count, 0, False))  1.28 us
    ppermute x1, starting transfers between devices, local(): lon_b = lax.ppermute(to_b, 'lon', swaps(lon_count, 1, True))  1.16 us
  transfers between devices with their start and end apart: 4, of which 1 were waited for; matrix products, arithmetic and copies ran while one was open for 0% of the time, Pallas kernels for 39%

profile of v2, /device:TPU:17, one launch (start us, length us, event | category | flops | bytes accessed | tf_op | source)
XLA Modules:
  0.0 20.6 jit_solution(1981070200770333543)
XLA Ops:
  0.6 1.0 %edge_rows.1 = (f32[192,128]{1,0:T(8,128)S(1)}, f32[192,128]{1,0:T(8,128)S(1)}) custom-call(f32[128,128]{1,0:T(8,128)} %bitcast.10, f32[128,128]{1,0:T(8,128)} %bitcast.12, f32[128,128]{1,0:T(8,128)} %bitcast.14, f32[128,128]{1,0:T(8,128)} %bitcast.16), custom_call_target="tpu_custom_call" | custom-call | tf_op jit(solution)/shard_map/edge_rows/pallas_call | solution.py:61
  1.6 1.3 %collective-permute-start = (f32[192,128]{1,0:T(8,128)S(1)}, f32[192,128]{1,0:T(8,128)S(1)}, u32[]{:S(2)}, u32[]{:S(2)}) collective-permute-start(f32[192,128]{1,0:T(8,128)S(1)} %get-tuple-element.27), channel_id=1, source_target_pairs={{0,1},{1,0},{2,3},{3,2},{4,5},{5,4},{6,7},{7,6},{8,9},{9,8},{10,11... | collective-permute-start | bytes 294920 | tf_op jit(solution)/shard_map/ppermute | solution.py:476
  2.9 2.0 %collective-permute-start.1 = (f32[192,128]{1,0:T(8,128)S(1)}, f32[192,128]{1,0:T(8,128)S(1)}, u32[]{:S(2)}, u32[]{:S(2)}) collective-permute-start(f32[192,128]{1,0:T(8,128)S(1)} %get-tuple-element.28), channel_id=1, source_target_pairs={{1,2},{2,1},{3,4},{4,3},{5,6},{6,5},{9,10},{10,9},{11,12},{12,11},... | collective-permute-start | bytes 294920 | tf_op jit(solution)/shard_map/ppermute | solution.py:475
  5.6 1.7 %prepare.1 = (f32[128,128]{1,0:T(8,128)S(1)}, bf16[256,512]{1,0:T(8,128)(2,1)S(1)}, bf16[2,112,128]{2,1,0:T(8,128)(2,1)S(1)}, bf16[3,32,16,128]{3,2,1,0:T(8,128)...) custom-call(f32[128,128]{1,0:T(8,128)} %bitcast.11, ...), custom_call_target="tpu_custom_call" | custom-call | flops 4194304 | bytes 2097152 | tf_op jit(solution)/shard_map/prepare/pallas_call | solution.py:175
  7.3 0.0 collective-permute-done.from_a.lat_a
  7.3 1.8 %collective-permute-done.1.from_b.lat_b = f32[192,128]{1,0:T(8,128)S(1)} collective-permute-done((f32[192,128]{1,0:T(8,128)S(1)}, f32[192,128]{1,0:T(8,128)S(1)}, u32[]{:S(2)}, u32[]{:S(2)}) %collective-permute-start.1) | collective-permute-done | bytes 98336 | tf_op jit(solution)/shard_map/ppermute | solution.py:475
  9.1 0.3 %edge_columns.1 = (f32[16,128]{1,0:T(8,128)S(1)}, f32[8,128]{1,0:T(8,128)S(1)}, f32[8,128]{1,0:T(8,128)S(1)}) custom-call(f32[256,128]{1,0:T(8,128)S(1)} %get-tuple-element.22.ft, f32[256,128]{1,0:T(8,128)S(1)} %get-tuple-element.23.fq, f32[16,128]{1,0:T(8,128)S(1)} %get-tuple-element.26.own, f32[192,128]{1,0:T(8,128)S(1)} %collective-permute-done.from_a.lat_a, ...), custom_call_target="tpu_custom_call" | custom-call | tf_op jit(solution)/shard_map/edge_columns/pallas_call | solution.py:228
  9.4 2.1 %collective-permute-start.2 = (f32[8,128]{1,0:T(8,128)S(1)}, f32[8,128]{1,0:T(8,128)S(1)}, u32[]{:S(2)}, u32[]{:S(2)}) collective-permute-start(f32[8,128]{1,0:T(8,128)S(1)} %get-tuple-element.30), channel_id=1, source_target_pairs={{0,8},{8,0},{16,24},{24,16},{1,9},{9,1},{17,25},{25,17},{2,10},{10... | collective-permute-start | bytes 12296 | tf_op jit(solution)/shard_map/ppermute | solution.py:492
  11.6 1.2 %collective-permute-start.3 = (f32[8,128]{1,0:T(8,128)S(1)}, f32[8,128]{1,0:T(8,128)S(1)}, u32[]{:S(2)}, u32[]{:S(2)}) collective-permute-start(f32[8,128]{1,0:T(8,128)S(1)} %get-tuple-element.31), channel_id=1, source_target_pairs={{8,16},{16,8},{24,0},{0,24},{9,17},{17,9},{25,1},{1,25},{10,18},{1... | collective-permute-start | bytes 12296 | tf_op jit(solution)/shard_map/ppermute | solution.py:491
  12.7 6.2 %heating.1 = f32[128,128]{1,0:T(8,128)} custom-call(f32[128,128]{1,0:T(8,128)S(1)} %get-tuple-element.34.factor, bf16[256,512]{1,0:T(8,128)(2,1)S(1)} %get-tuple-element.35.linear, bf16[2,112,128]{2,1,0:T(8,128)(2,1)S(1)} %get-tuple-element.36.tables, bf16[3,32,16,128]{3,2,1,0:T(8,128)(2,1)S(1)} %get-tuple-element.37.masks, ...), custom_call_target="tpu_custom_call" | custom-call | flops 1174405120 | bytes 1048576 | tf_op jit(solution)/shard_map/heating/pallas_call | solution.py:444
  19.0 0.0 collective-permute-done.2.lon_a
  19.0 0.0 collective-permute-done.3.lon_b
  19.0 1.6 %advect.1 = (f32[128,128]{1,0:T(8,128)}, f32[128,128]{1,0:T(8,128)}) custom-call(f32[256,128]{1,0:T(8,128)S(1)} %get-tuple-element.22.ft, f32[256,128]{1,0:T(8,128)S(1)} %get-tuple-element.23.fq, f32[256,128]{1,0:T(8,128)S(1)} %get-tuple-element.24.fx, f32[256,128]{1,0:T(8,128)S(1)} %get-tuple-element.25.fy, f32[16,128]{1,0:T(8,128)S(1)} %get-tuple-element.29.edges, ...), custom_call_target="tpu_custom_call" | custom-call | tf_op jit(solution)/shard_map/advect/pallas_call | solution.py:336
Async XLA Ops:
  1.6 5.7 %collective-permute-start = (f32[192,128]{1,0:T(8,128)S(1)}, f32[192,128]{1,0:T(8,128)S(1)}, u32[]{:S(2)}, u32[]{:S(2)}) collective-permute-start(f32[192,128]{1,0:T(8,128)S(1)} %get-tuple-element.27), channel_id=1, source_target_pairs={{0,1},{1,0},{2,3},{3,2},{4,5},{5,4},{6,7},{7,6},{8,9},{9,8},{10,11... | collective-permute-start | bytes 294920 | tf_op jit(solution)/shard_map/ppermute | solution.py:476
  2.9 6.2 %collective-permute-start.1 = (f32[192,128]{1,0:T(8,128)S(1)}, f32[192,128]{1,0:T(8,128)S(1)}, u32[]{:S(2)}, u32[]{:S(2)}) collective-permute-start(f32[192,128]{1,0:T(8,128)S(1)} %get-tuple-element.28), channel_id=1, source_target_pairs={{1,2},{2,1},{3,4},{4,3},{5,6},{6,5},{9,10},{10,9},{11,12},{12,11},... | collective-permute-start | bytes 294920 | tf_op jit(solution)/shard_map/ppermute | solution.py:475
  9.4 9.5 %collective-permute-start.2 = (f32[8,128]{1,0:T(8,128)S(1)}, f32[8,128]{1,0:T(8,128)S(1)}, u32[]{:S(2)}, u32[]{:S(2)}) collective-permute-start(f32[8,128]{1,0:T(8,128)S(1)} %get-tuple-element.30), channel_id=1, source_target_pairs={{0,8},{8,0},{16,24},{24,16},{1,9},{9,1},{17,25},{25,17},{2,10},{10... | collective-permute-start | bytes 12296 | tf_op jit(solution)/shard_map/ppermute | solution.py:492
  11.6 7.4 %collective-permute-start.3 = (f32[8,128]{1,0:T(8,128)S(1)}, f32[8,128]{1,0:T(8,128)S(1)}, u32[]{:S(2)}, u32[]{:S(2)}) collective-permute-start(f32[8,128]{1,0:T(8,128)S(1)} %get-tuple-element.31), channel_id=1, source_target_pairs={{8,16},{16,8},{24,0},{0,24},{9,17},{17,9},{25,1},{1,25},{10,18},{1... | collective-permute-start | bytes 12296 | tf_op jit(solution)/shard_map/ppermute | solution.py:491

commit v3 on v2

--- a/solution.py
+++ b/solution.py
@@ -41,28 +41,35 @@
     return pairs
 
 
-def rows_kernel(rows, t, q, cx, cy, to_a, to_b):
-    levels = t.shape[0] // rows
-    even = lax.rem(lax.axis_index("lat"), 2) == 0
-
-    def row(ref, r):
-        return ref[pl.ds(r, levels, stride=rows), :]
-
-    picks = ((t, 0), (t, 1), (q, 0), (q, 1), (cx, 0), (cy, 0))
-    for k, (ref, deep) in enumerate(picks):
-        high, low = row(ref, rows - 1 - deep), row(ref, deep)
-        to_a[k * levels : (k + 1) * levels, :] = jnp.where(even, high, low)
-        to_b[k * levels : (k + 1) * levels, :] = jnp.where(even, low, high)
+def odd_swaps(lat_count, lon_count):
+    pairs = []
+    for lon in range(lon_count):
+        pairs += [(lon * lat_count + i, lon * lat_count + j) for i, j in swaps(lat_count, 1, False)]
+        beside = lon + 1 if lon % 2 == 0 else lon - 1
+        ends = {0} | ({lat_count - 1} if lat_count % 2 == 0 else set())
+        pairs += [(lon * lat_count + end, beside * lat_count + end) for end in sorted(ends)]
+    return pairs
+
+
+def put_rows(blocks, rows, high_side, out):
+    levels = blocks[0].shape[0] // rows
+    t, q, cx, cy = blocks
+    for k, (ref, deep) in enumerate(((t, 0), (t, 1), (q, 0), (q, 1), (cx, 0), (cy, 0))):
+        high, low = (ref[pl.ds(r, levels, stride=rows), :] for r in (rows - 1 - deep, deep))
+        out[k * levels : (k + 1) * levels, :] = jnp.where(high_side, high, low)
+
+
+def rows_kernel(rows, t, q, cx, cy, to_a):
+    put_rows((t, q, cx, cy), rows, lax.rem(lax.axis_index("lat"), 2) == 0, to_a)
 
 
 def edge_rows(t, q, cx, cy, rows):
     total, lanes = t.shape
-    shape = (6 * (total // rows), lanes)
     return pl.pallas_call(
         functools.partial(rows_kernel, rows),
-        out_shape=(HELD(shape, f32),) * 2,
+        out_shape=HELD((6 * (total // rows), lanes), f32),
         in_specs=[VMEM_SPEC] * 4,
-        out_specs=(VMEM_SPEC,) * 2,
+        out_specs=VMEM_SPEC,
         name="edge_rows",
     )(t, q, cx, cy)
 
@@ -102,12 +109,13 @@
 
 def prepare_kernel(
     pad, t, q, cx, cy, mu, k, albedo, solar, tally, perm,
-    factor, linear, tables, masks, shares, albedos, scale, ft, fq, fx, fy, own,
+    to_b, factor, linear, tables, masks, shares, albedos, scale, ft, fq, fx, fy, own,
 ):
     levels, gpoints = k.shape
     rows, lanes = mu.shape
     tall = rows + 2 * pad
     blocks = (t, q, cx, cy)
+    put_rows(blocks, rows, lax.rem(lax.axis_index("lat"), 2) == 1, to_b)
     for ref, out in zip(blocks, (ft, fq, fx, fy)):
         for r in range(rows):
             out[pl.ds(pad + r, levels, stride=tall), :] = ref[pl.ds(r, levels, stride=rows), :]
@@ -175,6 +183,7 @@
     return pl.pallas_call(
         functools.partial(prepare_kernel, pad),
         out_shape=(
+            HELD((6 * levels, lanes), f32),
             HELD(t.shape, f32),
             HELD((2 * lanes, rows * lanes), bf16),
             HELD((2, gpoints, lanes), bf16),
@@ -186,7 +195,7 @@
             HELD((16, levels * rows), f32),
         ),
         in_specs=[VMEM_SPEC] * 8 + [SMEM_SPEC, VMEM_SPEC],
-        out_specs=(VMEM_SPEC,) * 12,
+        out_specs=(VMEM_SPEC,) * 13,
         cost_estimate=pl.CostEstimate(flops=1 << 22, bytes_accessed=1 << 21, transcendentals=1 << 17),
         name="prepare",
     )(t, q, cx, cy, mu, k, albedo, solar, tally, perm)
@@ -203,7 +212,7 @@
     return lax.rem(lat, 2) == 0, lat == 0, lat == lax.axis_size("lat") - 1
 
 
-def columns_kernel(pad, ft, fq, own, from_a, from_b, edges, to_a, to_b, ring):
+def columns_kernel(pad, ft, fq, own, from_a, from_b, _, edges, to_a, to_b, ring):
     levels = from_a.shape[0] // 6
     total, lanes = ring.shape[1:]
     rows = total // levels
@@ -222,17 +231,17 @@
     to_b[...] = jnp.where(even_lon, west, east)
 
 
-def edge_columns(ft, fq, own, from_a, from_b, rows, pad):
+def edge_columns(ft, fq, own, from_a, from_b, after, rows, pad):
     lanes = ft.shape[1]
     total = own.shape[1]
     return pl.pallas_call(
         functools.partial(columns_kernel, pad),
         out_shape=(HELD((16, total), f32), HELD((8, total), f32), HELD((8, total), f32)),
-        in_specs=[VMEM_SPEC] * 5,
+        in_specs=[VMEM_SPEC] * 6,
         out_specs=(VMEM_SPEC,) * 3,
         scratch_shapes=[pltpu.VMEM((2, total, lanes), f32)],
         name="edge_columns",
-    )(*held(ft, fq, own, from_a, from_b))
+    )(*held(ft, fq, own, from_a, from_b, after))
 
 
 def weights(cx, cy):
@@ -343,16 +352,22 @@
     )(*held(ft, fq, fx, fy, edges, lat_a, lat_b, lon_a, lon_b))
 
 SLOTS, AHEAD = 16, 8
+EARLY = 5
 
 
 def heating_kernel(
-    factor, linear, tables, masks, shares, albedos, scale, out, trans, pull, beam, total
+    begin, end, linear, tables, masks, shares, albedos, *refs
 ):
     gpoints, levels = shares.shape
-    rows, lanes = scale.shape
+    lanes = albedos.shape[1]
+    rows = linear.shape[1] // lanes
+    if begin == 0:
+        total, trans, pull, beam = refs
+    else:
+        so_far, factor, scale, _, out, trans, pull, beam, total = refs
     wide = 2 * lanes
     engines = rows // 2
-    total[...] = jnp.zeros_like(total)
+    total[...] = jnp.zeros_like(total) if begin == 0 else so_far[...]
     units = [(a, b) for a in range(2) for b in range(rows)]
     each = range(len(units))
 
@@ -423,33 +438,38 @@
             pltpu.matmul_push_rhs(linear[:, m * wide : (m + 1) * wide], 0, m)
             pltpu.matmul_acc_lhs(last, nothing, load_staged_rhs=0)
             pltpu.matmul_pop(last)
-        pl.loop(0, gpoints // 16)(group)
+        pl.loop(begin, end)(group)
 
     pl.run_scoped(
         main,
         *[pltpu.ACC(m)((48, wide), f32) for m in range(engines) for _ in range(SLOTS)],
         *[pltpu.ACC(m)((16, wide), f32) for m in range(engines)],
     )
+    if begin == 0:
+        return
     column_scale = scale[...]
     for l in range(levels):
         here = pl.ds(l * rows, rows)
         out[here, :] = jnp.sum(total[l], axis=1) * column_scale * factor[here, :]
 
 
-def heating(factor, linear, tables, masks, shares, albedos, scale):
-    rows, lanes = scale.shape
+def heating(linear, tables, masks, shares, albedos, begin, end, more=()):
     gpoints, levels = shares.shape
+    lanes = albedos.shape[1]
+    rows = linear.shape[1] // lanes
     stage = pltpu.VMEM((2 * rows, levels, 8, lanes), f32)
-    cells = gpoints * levels * rows * lanes
+    sums = (levels, rows, 8, lanes)
+    cells = (end - begin) * 16 * levels * rows * lanes
     return pl.pallas_call(
-        heating_kernel,
-        out_shape=shape_of(levels * rows, lanes),
-        in_specs=[VMEM_SPEC] * 7,
+        functools.partial(heating_kernel, begin, end),
+        out_shape=shape_of(levels * rows, lanes) if more else HELD(sums, f32),
+        in_specs=[VMEM_SPEC] * (5 + len(more)),
         out_specs=VMEM_SPEC,
-        scratch_shapes=[stage, stage, stage, pltpu.VMEM((levels, rows, 8, lanes), f32)],
+        scratch_shapes=[stage, stage, stage] + [pltpu.VMEM(sums, f32)] * bool(more),
         cost_estimate=pl.CostEstimate(flops=640 * cells, bytes_accessed=1 << 20, transcendentals=2 * cells),
         name="heating",
-    )(*held(factor, linear, tables, masks, shares, albedos, scale))
+    )(*held(linear, tables, masks, shares, albedos, *more))
+
 
 def local(
     thermal_deviation,
@@ -471,10 +491,9 @@
         flat(x)
         for x in (thermal_deviation, moisture_deviation, eastward_stability, northward_stability)
     )
-    to_a, to_b = edge_rows(t, q, cx, cy, rows)
-    lat_b = lax.ppermute(to_b, "lat", swaps(lat_count, 1, False))
+    to_a = edge_rows(t, q, cx, cy, rows)
     lat_a = lax.ppermute(to_a, "lat", swaps(lat_count, 0, False))
-    *tables, ft, fq, fx, fy, own = prepare(
+    to_b, factor, *tables, scale, ft, fq, fx, fy, own = prepare(
         t,
         q,
         cx,
@@ -487,10 +506,14 @@
         daylight_permutation,
         pad,
     )
-    edges, to_a, to_b = edge_columns(ft, fq, own, lat_a, lat_b, rows, pad)
+    lat_b = lax.ppermute(to_b, ("lon", "lat"), odd_swaps(lat_count, lon_count))
+    groups = extinction_coeff.shape[0] // 16
+    early = min(EARLY, groups - 1)
+    sums = heating(*tables, 0, early)
+    edges, to_a, to_b = edge_columns(ft, fq, own, lat_a, lat_b, sums, rows, pad)
     lon_b = lax.ppermute(to_b, "lon", swaps(lon_count, 1, True))
     lon_a = lax.ppermute(to_a, "lon", swaps(lon_count, 0, True))
-    warming = heating(*tables)
+    warming = heating(*tables, early, groups, (sums, factor, scale, edges))
     t_next, q_next = advect(ft, fq, fx, fy, edges, lat_a, lat_b, lon_a, lon_b, rows, pad)
     whole = lambda x: x.reshape(levels, rows, lanes)
     return whole(t_next), whole(q_next), whole(warming)

time: 20.8 us -> 17.7 us (0.85)
  the two profiles are of different devices: /device:TPU:17 before, /device:TPU:3 now
where the time goes in v3:
time: 17.7 us; the launch traced here: 17.4 us
  Pallas kernels  11.1 us (63%)
  starting transfers between devices  4.96 us (28%)
  between operations  1.32 us (7%)
    pallas_call x2, Pallas kernels, heating(): pl.pallas_call(functools.partial(heating_kernel, begin, end), out_shape=s...  6.53 us
    ppermute x1, starting transfers between devices, local(): lat_b = lax.ppermute(to_b, ('lon', 'lat'), odd_swaps(lat_count, lon_count))  2.48 us
    pallas_call x1, Pallas kernels, prepare(): pl.pallas_call(functools.partial(prepare_kernel, pad), out_shape=(HELD((6...  1.7 us
    pallas_call x1, Pallas kernels, advect(): pl.pallas_call(functools.partial(advect_kernel, rows, pad), out_shape=(sh...  1.62 us
    ppermute x1, starting transfers between devices, local(): lon_a = lax.ppermute(to_a, 'lon', swaps(lon_count, 0, True))  1.25 us
    ppermute x1, starting transfers between devices, local(): lon_b = lax.ppermute(to_b, 'lon', swaps(lon_count, 1, True))  1.16 us
    pallas_call x1, Pallas kernels, edge_rows(): pl.pallas_call(functools.partial(rows_kernel, rows), out_shape=HELD((6 *...  0.96 us
  transfers between devices with their start and end apart: 4, of which 0 were waited for; matrix products, arithmetic and copies ran while one was open for 0% of the time, Pallas kernels for 47%

profile of v3, /device:TPU:3, one launch (start us, length us, event | category | flops | bytes accessed | tf_op | source)
XLA Modules:
  0.0 17.4 jit_solution(9153755475479409638)
XLA Ops:
  0.6 1.0 %edge_rows.1 = f32[192,128]{1,0:T(8,128)S(1)} custom-call(f32[128,128]{1,0:T(8,128)} %bitcast.10, f32[128,128]{1,0:T(8,128)} %bitcast.12, f32[128,128]{1,0:T(8,128)} %bitcast.14, f32[128,128]{1,0:T(8,128)} %bitcast.16), custom_call_target="tpu_custom_call" | custom-call | tf_op jit(solution)/shard_map/edge_rows/pallas_call | solution.py:68
  1.6 0.1 collective-permute-start
  2.3 1.7 %prepare.1 = (f32[192,128]{1,0:T(8,128)S(1)}, f32[128,128]{1,0:T(8,128)S(1)}, bf16[256,512]{1,0:T(8,128)(2,1)S(1)}, bf16[2,112,128]{2,1,0:T(8,128)(2,1)S(1)}, bf...) custom-call(f32[128,128]{1,0:T(8,128)} %bitcast.11, ...), custom_call_target="tpu_custom_call" | custom-call | flops 4194304 | bytes 2097152 | tf_op jit(solution)/shard_map/prepare/pallas_call | solution.py:183
  4.0 2.5 %collective-permute-start.1 = (f32[192,128]{1,0:T(8,128)S(1)}, f32[192,128]{1,0:T(8,128)S(1)}, u32[]{:S(2)}, u32[]{:S(2)}) collective-permute-start(f32[192,128]{1,0:T(8,128)S(1)} %get-tuple-element.26), channel_id=1, source_target_pairs={{1,2},{2,1},{3,4},{4,3},{5,6},{6,5},{0,8},{7,15},{9,10},{10,9},{11... | collective-permute-start | bytes 294920 | tf_op jit(solution)/shard_map/ppermute | solution.py:509
  6.5 4.1 %heating.2._.refs_0_ = f32[32,4,8,128]{3,2,1,0:T(8,128)S(1)} custom-call(bf16[256,512]{1,0:T(8,128)(2,1)S(1)} %get-tuple-element.27.linear, bf16[2,112,128]{2,1,0:T(8,128)(2,1)S(1)} %get-tuple-element.28.tables, bf16[3,32,16,128]{3,2,1,0:T(8,128)(2,1)S(1)} %get-tuple-element.29.masks, f32[112,32]{1,0:T(8,128)S(1)} %get-tuple-element.30.shares, ...), custom_call_target="tpu_custom_call" | custom-call | flops 838860800 | bytes 1048576 | tf_op jit(solution)/shard_map/heating/pallas_call | solution.py:463
  10.6 0.0 collective-permute-done.from_a.lat_a
  10.6 0.0 collective-permute-done.1.from_b.lat_b
  10.6 0.3 %edge_columns.1 = (f32[16,128]{1,0:T(8,128)S(1)}, f32[8,128]{1,0:T(8,128)S(1)}, f32[8,128]{1,0:T(8,128)S(1)}) custom-call(f32[256,128]{1,0:T(8,128)S(1)} %get-tuple-element.21.ft, f32[256,128]{1,0:T(8,128)S(1)} %get-tuple-element.22.fq, f32[16,128]{1,0:T(8,128)S(1)} %get-tuple-element.25.own, f32[192,128]{1,0:T(8,128)S(1)} %collective-permute-done.from_a.lat_a, ...), custom_call_target="tpu_custom_call" | custom-call | tf_op jit(solution)/shard_map/edge_columns/pallas_call | solution.py:237
  10.9 1.3 %collective-permute-start.2 = (f32[8,128]{1,0:T(8,128)S(1)}, f32[8,128]{1,0:T(8,128)S(1)}, u32[]{:S(2)}, u32[]{:S(2)}) collective-permute-start(f32[8,128]{1,0:T(8,128)S(1)} %get-tuple-element.33), channel_id=1, source_target_pairs={{0,8},{8,0},{16,24},{24,16},{1,9},{9,1},{17,25},{25,17},{2,10},{10... | collective-permute-start | bytes 12296 | tf_op jit(solution)/shard_map/ppermute | solution.py:515
  12.2 1.2 %collective-permute-start.3 = (f32[8,128]{1,0:T(8,128)S(1)}, f32[8,128]{1,0:T(8,128)S(1)}, u32[]{:S(2)}, u32[]{:S(2)}) collective-permute-start(f32[8,128]{1,0:T(8,128)S(1)} %get-tuple-element.34), channel_id=1, source_target_pairs={{8,16},{16,8},{24,0},{0,24},{9,17},{17,9},{25,1},{1,25},{10,18},{1... | collective-permute-start | bytes 12296 | tf_op jit(solution)/shard_map/ppermute | solution.py:514
  13.3 2.5 %heating.3 = f32[128,128]{1,0:T(8,128)} custom-call(bf16[256,512]{1,0:T(8,128)(2,1)S(1)} %get-tuple-element.27.linear, bf16[2,112,128]{2,1,0:T(8,128)(2,1)S(1)} %get-tuple-element.28.tables, bf16[3,32,16,128]{3,2,1,0:T(8,128)(2,1)S(1)} %get-tuple-element.29.masks, f32[112,32]{1,0:T(8,128)S(1)} %get-tuple-element.30.shares, ...), custom_call_target="tpu_custom_call" | custom-call | flops 335544320 | bytes 1048576 | tf_op jit(solution)/shard_map/heating/pallas_call | solution.py:463
  15.8 0.0 collective-permute-done.2.lon_a
  15.8 0.0 collective-permute-done.3.lon_b
  15.8 1.6 %advect.1 = (f32[128,128]{1,0:T(8,128)}, f32[128,128]{1,0:T(8,128)}) custom-call(f32[256,128]{1,0:T(8,128)S(1)} %get-tuple-element.21.ft, f32[256,128]{1,0:T(8,128)S(1)} %get-tuple-element.22.fq, f32[256,128]{1,0:T(8,128)S(1)} %get-tuple-element.23.fx, f32[256,128]{1,0:T(8,128)S(1)} %get-tuple-element.24.fy, f32[16,128]{1,0:T(8,128)S(1)} %get-tuple-element.32.edges.refs_3_, ...), custom_call_target="tpu_custom_call" | custom-call | tf_op jit(solution)/shard_map/advect/pallas_call | solution.py:345
Async XLA Ops:
  1.6 9.0 %collective-permute-start = (f32[192,128]{1,0:T(8,128)S(1)}, f32[192,128]{1,0:T(8,128)S(1)}, u32[]{:S(2)}, u32[]{:S(2)}) collective-permute-start(f32[192,128]{1,0:T(8,128)S(1)} %edge_rows.1), channel_id=1, source_target_pairs={{0,1},{1,0},{2,3},{3,2},{4,5},{5,4},{6,7},{7,6},{8,9},{9,8},{10,11... | collective-permute-start | bytes 294920 | tf_op jit(solution)/shard_map/ppermute | solution.py:495
  4.0 6.6 %collective-permute-start.1 = (f32[192,128]{1,0:T(8,128)S(1)}, f32[192,128]{1,0:T(8,128)S(1)}, u32[]{:S(2)}, u32[]{:S(2)}) collective-permute-start(f32[192,128]{1,0:T(8,128)S(1)} %get-tuple-element.26), channel_id=1, source_target_pairs={{1,2},{2,1},{3,4},{4,3},{5,6},{6,5},{0,8},{7,15},{9,10},{10,9},{11... | collective-permute-start | bytes 294920 | tf_op jit(solution)/shard_map/ppermute | solution.py:509
  10.9 4.9 %collective-permute-start.2 = (f32[8,128]{1,0:T(8,128)S(1)}, f32[8,128]{1,0:T(8,128)S(1)}, u32[]{:S(2)}, u32[]{:S(2)}) collective-permute-start(f32[8,128]{1,0:T(8,128)S(1)} %get-tuple-element.33), channel_id=1, source_target_pairs={{0,8},{8,0},{16,24},{24,16},{1,9},{9,1},{17,25},{25,17},{2,10},{10... | collective-permute-start | bytes 12296 | tf_op jit(solution)/shard_map/ppermute | solution.py:515
  12.2 3.6 %collective-permute-start.3 = (f32[8,128]{1,0:T(8,128)S(1)}, f32[8,128]{1,0:T(8,128)S(1)}, u32[]{:S(2)}, u32[]{:S(2)}) collective-permute-start(f32[8,128]{1,0:T(8,128)S(1)} %get-tuple-element.34), channel_id=1, source_target_pairs={{8,16},{16,8},{24,0},{0,24},{9,17},{17,9},{25,1},{1,25},{10,18},{1... | collective-permute-start | bytes 12296 | tf_op jit(solution)/shard_map/ppermute | solution.py:514

commit v4 on v3

--- a/solution.py
+++ b/solution.py
@@ -59,19 +59,28 @@
         out[k * levels : (k + 1) * levels, :] = jnp.where(high_side, high, low)
 
 
-def rows_kernel(rows, t, q, cx, cy, to_a):
-    put_rows((t, q, cx, cy), rows, lax.rem(lax.axis_index("lat"), 2) == 0, to_a)
-
-
-def edge_rows(t, q, cx, cy, rows):
-    total, lanes = t.shape
-    return pl.pallas_call(
+def rows_kernel(rows, tally, perm, *refs):
+    count = (len(refs) - 3) // 2
+    inputs, (to_a, to_b, sunlit), copies = refs[:count], refs[count : count + 3], refs[count + 3 :]
+    even = lax.rem(lax.axis_index("lat"), 2) == 0
+    put_rows(inputs[:4], rows, even, to_a)
+    put_rows(inputs[:4], rows, jnp.logical_not(even), to_b)
+    sunlit[...] = jnp.where(iota(perm.shape, 2) < tally[0, 0], perm[...], -1)
+    for ref, copy in zip(inputs, copies):
+        copy[...] = ref[...]
+
+
+def edge_rows(rows, tally, perm, *arrays):
+    total, lanes = arrays[0].shape
+    sent = HELD((6 * (total // rows), lanes), f32)
+    to_a, to_b, sunlit, *copies = pl.pallas_call(
         functools.partial(rows_kernel, rows),
-        out_shape=HELD((6 * (total // rows), lanes), f32),
-        in_specs=[VMEM_SPEC] * 4,
-        out_specs=VMEM_SPEC,
+        out_shape=(sent, sent, *(HELD(x.shape, x.dtype) for x in (perm, *arrays))),
+        in_specs=[SMEM_SPEC] + [VMEM_SPEC] * (1 + len(arrays)),
+        out_specs=(VMEM_SPEC,) * (3 + len(arrays)),
         name="edge_rows",
-    )(t, q, cx, cy)
+    )(tally, perm, *arrays)
+    return to_a, to_b, (*copies, sunlit)
 
 
 def halves(x):
@@ -108,27 +117,24 @@
 
 
 def prepare_kernel(
-    pad, t, q, cx, cy, mu, k, albedo, solar, tally, perm,
-    to_b, factor, linear, tables, masks, shares, albedos, scale, ft, fq, fx, fy, own,
+    pad, t, q, cx, cy, mu, k, albedo, solar, sunlit,
+    factor, linear, tables, masks, shares, albedos, scale, ft, fq, fx, fy, own,
 ):
     levels, gpoints = k.shape
     rows, lanes = mu.shape
     tall = rows + 2 * pad
     blocks = (t, q, cx, cy)
-    put_rows(blocks, rows, lax.rem(lax.axis_index("lat"), 2) == 1, to_b)
     for ref, out in zip(blocks, (ft, fq, fx, fy)):
         for r in range(rows):
             out[pl.ds(pad + r, levels, stride=tall), :] = ref[pl.ds(r, levels, stride=rows), :]
     own[...] = pick_edges(((0, 1), (2, 3), (4,), (5,)), lanes, [ref[...] for ref in blocks])
 
-    count = tally[0, 0]
     found = jnp.zeros((8, lanes), f32)
     for r in range(rows):
-        column = perm[0, :, r * lanes : (r + 1) * lanes]
-        row_at = column // lanes
-        lane_at = column - row_at * lanes
-        sunlit = iota((1, lanes), 1) + r * lanes < count
-        at_row = jnp.where((row_at == iota((8, lanes), 0)) & sunlit, 1.0, 0.0).astype(bf16)
+        column = sunlit[0, :, r * lanes : (r + 1) * lanes]
+        row_at = jnp.where(column < 0, -1, column // lanes)
+        lane_at = lax.rem(column, lanes)
+        at_row = jnp.where(row_at == iota((8, lanes), 0), 1.0, 0.0).astype(bf16)
         at_lane = jnp.where(lane_at == iota((lanes, lanes), 0), 1.0, 0.0).astype(bf16)
         found += lax.dot_general(at_row, at_lane, NT_DIMS, preferred_element_type=f32)
     scale[...] = heat_coeff * mu[...] * found[:rows]
@@ -176,14 +182,13 @@
         ).astype(bf16)
 
 
-def prepare(t, q, cx, cy, mu, k, albedo, solar, tally, perm, pad):
+def prepare(t, q, cx, cy, mu, k, albedo, solar, sunlit, pad):
     levels, gpoints = k.shape
     rows, lanes = mu.shape
     tall = levels * (rows + 2 * pad)
     return pl.pallas_call(
         functools.partial(prepare_kernel, pad),
         out_shape=(
-            HELD((6 * levels, lanes), f32),
             HELD(t.shape, f32),
             HELD((2 * lanes, rows * lanes), bf16),
             HELD((2, gpoints, lanes), bf16),
@@ -194,11 +199,11 @@
             *[HELD((tall, lanes), f32)] * 4,
             HELD((16, levels * rows), f32),
         ),
-        in_specs=[VMEM_SPEC] * 8 + [SMEM_SPEC, VMEM_SPEC],
-        out_specs=(VMEM_SPEC,) * 13,
+        in_specs=[VMEM_SPEC] * 9,
+        out_specs=(VMEM_SPEC,) * 12,
         cost_estimate=pl.CostEstimate(flops=1 << 22, bytes_accessed=1 << 21, transcendentals=1 << 17),
         name="prepare",
-    )(t, q, cx, cy, mu, k, albedo, solar, tally, perm)
+    )(*held(t, q, cx, cy, mu, k, albedo, solar, sunlit))
 
 
 def by_side(even, first, last, from_a, from_b, k, levels, low, high):
@@ -375,30 +380,30 @@
         def at(m, l):
             return sums[m * SLOTS + l % SLOTS]
 
+        blank = jnp.zeros((16, lanes), bf16)
+
+        def issue(i, l):
+            start = pl.multiple_of(i * 16, 16)
+            plain, absorbing = (tables[j, pl.ds(start, 16), :] for j in range(2))
+            stack = [
+                jnp.concatenate([plain * masks[0, l], blank], axis=1),
+                jnp.concatenate([absorbing * masks[1, l], blank], axis=1),
+                jnp.concatenate([blank, plain * masks[2, l]], axis=1),
+            ]
+            stack = jnp.concatenate(stack, axis=0)
+            for m in range(engines):
+                pltpu.matmul_acc_lhs(at(m, l), stack)
+
         def group(i):
             start = pl.multiple_of(i * 16, 16)
             starts = [pl.multiple_of(start + 8 * a, 8) for a in range(2)]
-            plain, absorbing = (tables[j, pl.ds(start, 16), :] for j in range(2))
             w15 = [albedos[pl.ds(s, 8), :] for s in starts]
             share = [shares[pl.ds(s, 8), :] for s in starts]
-            blank = jnp.zeros((16, lanes), bf16)
-
-            def issue(l):
-                stack = [
-                    jnp.concatenate([plain * masks[0, l], blank], axis=1),
-                    jnp.concatenate([absorbing * masks[1, l], blank], axis=1),
-                    jnp.concatenate([blank, plain * masks[2, l]], axis=1),
-                ]
-                stack = jnp.concatenate(stack, axis=0)
-                for m in range(engines):
-                    pltpu.matmul_acc_lhs(at(m, l), stack)
-
-            for l in range(AHEAD):
-                issue(l)
+            following = jnp.minimum(i + 1, end - 1)
             y = current = step = None
             for l in range(levels):
                 if l + AHEAD < levels:
-                    issue(l + AHEAD)
+                    issue(i, l + AHEAD)
                 popped = [pltpu.matmul_pop(at(m, l)) for m in range(engines)]
 
                 def part(kind, a, b):
@@ -422,6 +427,8 @@
                         pull[u, l] = resist[u] * current[u]
             diffuse = [current[u] / y[u] for u in each]
             for l in range(levels - 1, -1, -1):
+                if levels - 1 - l < AHEAD:
+                    issue(following, levels - 1 - l)
                 if l < levels - 1:
                     diffuse = [trans[u, l] * (pull[u, l] + diffuse[u]) for u in each]
                 spread = [jnp.broadcast_to(share[a][:, l : l + 1], (8, lanes)) for a in range(2)]
@@ -438,7 +445,12 @@
             pltpu.matmul_push_rhs(linear[:, m * wide : (m + 1) * wide], 0, m)
             pltpu.matmul_acc_lhs(last, nothing, load_staged_rhs=0)
             pltpu.matmul_pop(last)
+        for l in range(AHEAD):
+            issue(begin, l)
         pl.loop(begin, end)(group)
+        for l in range(AHEAD):
+            for m in range(engines):
+                pltpu.matmul_pop(at(m, l))
 
     pl.run_scoped(
         main,
@@ -491,9 +503,10 @@
         flat(x)
         for x in (thermal_deviation, moisture_deviation, eastward_stability, northward_stability)
     )
-    to_a = edge_rows(t, q, cx, cy, rows)
-    lat_a = lax.ppermute(to_a, "lat", swaps(lat_count, 0, False))
-    to_b, factor, *tables, scale, ft, fq, fx, fy, own = prepare(
+    to_a, to_b, copies = edge_rows(
+        rows,
+        daylight_tally,
+        daylight_permutation,
         t,
         q,
         cx,
@@ -502,11 +515,10 @@
         jnp.transpose(extinction_coeff),
         reflectivity_ratio.reshape(1, -1),
         insolation_source.reshape(1, -1),
-        daylight_tally,
-        daylight_permutation,
-        pad,
     )
+    lat_a = lax.ppermute(to_a, "lat", swaps(lat_count, 0, False))
     lat_b = lax.ppermute(to_b, ("lon", "lat"), odd_swaps(lat_count, lon_count))
+    factor, *tables, scale, ft, fq, fx, fy, own = prepare(*copies, pad)
     groups = extinction_coeff.shape[0] // 16
     early = min(EARLY, groups - 1)
     sums = heating(*tables, 0, early)

time: 17.7 us -> 16.5 us (0.932)
  Pallas kernels: 11.1 us -> 10.1 us
    pallas_call x2, Pallas kernels: 2.66 us -> 1.7 us  [the longest x1 1.04 us: edge_rows(): pl.pallas_call(functools.partial(rows_kernel, rows), out_shape=(sent, sen...]
  transfers between devices with their start and end apart: 4 -> 4, of which waited for: 0 -> 0; matrix products, arithmetic and copies ran while one was open for 0% -> 0% of each run, Pallas kernels for 47% -> 43%
where the time goes in v4:
time: 16.5 us; the launch traced here: 16.3 us
  Pallas kernels  10.1 us (61%)
  starting transfers between devices  4.95 us (30%)
  between operations  1.32 us (8%)
    pallas_call x2, Pallas kernels, heating(): pl.pallas_call(functools.partial(heating_kernel, begin, end), out_shape=s...  6.41 us
    ppermute x1, starting transfers between devices, local(): lat_b = lax.ppermute(to_b, ('lon', 'lat'), odd_swaps(lat_count, lon_count))  2.47 us
    pallas_call x1, Pallas kernels, advect(): pl.pallas_call(functools.partial(advect_kernel, rows, pad), out_shape=(sh...  1.63 us
    ppermute x1, starting transfers between devices, local(): lon_a = lax.ppermute(to_a, 'lon', swaps(lon_count, 0, True))  1.26 us
    ppermute x1, starting transfers between devices, local(): lon_b = lax.ppermute(to_b, 'lon', swaps(lon_count, 1, True))  1.15 us
    pallas_call x1, Pallas kernels, edge_rows(): pl.pallas_call(functools.partial(rows_kernel, rows), out_shape=(sent, sen...  1.04 us
    pallas_call x1, Pallas kernels, prepare(): pl.pallas_call(functools.partial(prepare_kernel, pad), out_shape=(HELD(t....  0.66 us
  transfers between devices with their start and end apart: 4, of which 0 were waited for; matrix products, arithmetic and copies ran while one was open for 0% of the time, Pallas kernels for 43%

profile of v4, /device:TPU:3, one launch (start us, length us, event | category | flops | bytes accessed | tf_op | source)
XLA Modules:
  0.0 16.3 jit_solution(5555201743225704120)
XLA Ops:
  1.3 1.0 %edge_rows.1 = (f32[192,128]{1,0:T(8,128)S(1)}, f32[192,128]{1,0:T(8,128)S(1)}, s32[1,1,512]{2,1,0:T(1,128)S(1)}, f32[128,128]{1,0:T(8,128)S(1)}, f32[128,128]{1...) custom-call(s32[1,1]{1,0:T(1,128)S(6)} %copy.13.tally, ...), custom_call_target="tpu_custom_call" | custom-call | tf_op jit(solution)/shard_map/edge_rows/pallas_call | solution.py:76
  2.3 0.1 collective-permute-start
  2.4 2.5 %collective-permute-start.1 = (f32[192,128]{1,0:T(8,128)S(1)}, f32[192,128]{1,0:T(8,128)S(1)}, u32[]{:S(2)}, u32[]{:S(2)}) collective-permute-start(f32[192,128]{1,0:T(8,128)S(1)} %get-tuple-element.46), channel_id=1, source_target_pairs={{1,2},{2,1},{3,4},{4,3},{5,6},{6,5},{0,8},{7,15},{9,10},{10,9},{11... | collective-permute-start | bytes 294920 | tf_op jit(solution)/shard_map/ppermute | solution.py:520
  4.9 0.7 %prepare.1 = (f32[128,128]{1,0:T(8,128)S(1)}, bf16[256,512]{1,0:T(8,128)(2,1)S(1)}, bf16[2,112,128]{2,1,0:T(8,128)(2,1)S(1)}, bf16[3,32,16,128]{3,2,1,0:T(8,128)...) custom-call(f32[128,128]{1,0:T(8,128)S(1)} %get-tuple-element.31.t, ...), custom_call_target="tpu_custom_call" | custom-call | flops 4194304 | bytes 2097152 | tf_op jit(solution)/shard_map/prepare/pallas_call | solution.py:189
  5.5 4.0 %heating.2._.refs_0_ = f32[32,4,8,128]{3,2,1,0:T(8,128)S(1)} custom-call(bf16[256,512]{1,0:T(8,128)(2,1)S(1)} %get-tuple-element.47.linear, bf16[2,112,128]{2,1,0:T(8,128)(2,1)S(1)} %get-tuple-element.48.tables, bf16[3,32,16,128]{3,2,1,0:T(8,128)(2,1)S(1)} %get-tuple-element.49.masks, f32[112,32]{1,0:T(8,128)S(1)} %get-tuple-element.50.shares, ...), custom_call_target="tpu_custom_call" | custom-call | flops 838860800 | bytes 1048576 | tf_op jit(solution)/shard_map/heating/pallas_call | solution.py:475
  9.5 0.0 collective-permute-done.from_a.lat_a
  9.5 0.0 collective-permute-done.1.from_b.lat_b
  9.6 0.3 %edge_columns.1 = (f32[16,128]{1,0:T(8,128)S(1)}, f32[8,128]{1,0:T(8,128)S(1)}, f32[8,128]{1,0:T(8,128)S(1)}) custom-call(f32[256,128]{1,0:T(8,128)S(1)} %get-tuple-element.40.ft, f32[256,128]{1,0:T(8,128)S(1)} %get-tuple-element.41.fq, f32[16,128]{1,0:T(8,128)S(1)} %get-tuple-element.44.own, f32[192,128]{1,0:T(8,128)S(1)} %collective-permute-done.from_a.lat_a, ...), custom_call_target="tpu_custom_call" | custom-call | tf_op jit(solution)/shard_map/edge_columns/pallas_call | solution.py:242
  9.9 1.3 %collective-permute-start.2 = (f32[8,128]{1,0:T(8,128)S(1)}, f32[8,128]{1,0:T(8,128)S(1)}, u32[]{:S(2)}, u32[]{:S(2)}) collective-permute-start(f32[8,128]{1,0:T(8,128)S(1)} %get-tuple-element.53), channel_id=1, source_target_pairs={{0,8},{8,0},{16,24},{24,16},{1,9},{9,1},{17,25},{25,17},{2,10},{10... | collective-permute-start | bytes 12296 | tf_op jit(solution)/shard_map/ppermute | solution.py:527
  11.2 1.1 %collective-permute-start.3 = (f32[8,128]{1,0:T(8,128)S(1)}, f32[8,128]{1,0:T(8,128)S(1)}, u32[]{:S(2)}, u32[]{:S(2)}) collective-permute-start(f32[8,128]{1,0:T(8,128)S(1)} %get-tuple-element.54), channel_id=1, source_target_pairs={{8,16},{16,8},{24,0},{0,24},{9,17},{17,9},{25,1},{1,25},{10,18},{1... | collective-permute-start | bytes 12296 | tf_op jit(solution)/shard_map/ppermute | solution.py:526
  12.3 2.4 %heating.3 = f32[128,128]{1,0:T(8,128)} custom-call(bf16[256,512]{1,0:T(8,128)(2,1)S(1)} %get-tuple-element.47.linear, bf16[2,112,128]{2,1,0:T(8,128)(2,1)S(1)} %get-tuple-element.48.tables, bf16[3,32,16,128]{3,2,1,0:T(8,128)(2,1)S(1)} %get-tuple-element.49.masks, f32[112,32]{1,0:T(8,128)S(1)} %get-tuple-element.50.shares, ...), custom_call_target="tpu_custom_call" | custom-call | flops 335544320 | bytes 1048576 | tf_op jit(solution)/shard_map/heating/pallas_call | solution.py:475
  14.7 0.0 collective-permute-done.2.lon_a
  14.7 0.0 collective-permute-done.3.lon_b
  14.7 1.6 %advect.1 = (f32[128,128]{1,0:T(8,128)}, f32[128,128]{1,0:T(8,128)}) custom-call(f32[256,128]{1,0:T(8,128)S(1)} %get-tuple-element.40.ft, f32[256,128]{1,0:T(8,128)S(1)} %get-tuple-element.41.fq, f32[256,128]{1,0:T(8,128)S(1)} %get-tuple-element.42.fx, f32[256,128]{1,0:T(8,128)S(1)} %get-tuple-element.43.fy, f32[16,128]{1,0:T(8,128)S(1)} %get-tuple-element.52.edges.refs_3_, ...), custom_call_target="tpu_custom_call" | custom-call | tf_op jit(solution)/shard_map/advect/pallas_call | solution.py:350
Async XLA Ops:
  2.3 7.2 %collective-permute-start = (f32[192,128]{1,0:T(8,128)S(1)}, f32[192,128]{1,0:T(8,128)S(1)}, u32[]{:S(2)}, u32[]{:S(2)}) collective-permute-start(f32[192,128]{1,0:T(8,128)S(1)} %get-tuple-element.45), channel_id=1, source_target_pairs={{0,1},{1,0},{2,3},{3,2},{4,5},{5,4},{6,7},{7,6},{8,9},{9,8},{10,11... | collective-permute-start | bytes 294920 | tf_op jit(solution)/shard_map/ppermute | solution.py:519
  2.4 7.2 %collective-permute-start.1 = (f32[192,128]{1,0:T(8,128)S(1)}, f32[192,128]{1,0:T(8,128)S(1)}, u32[]{:S(2)}, u32[]{:S(2)}) collective-permute-start(f32[192,128]{1,0:T(8,128)S(1)} %get-tuple-element.46), channel_id=1, source_target_pairs={{1,2},{2,1},{3,4},{4,3},{5,6},{6,5},{0,8},{7,15},{9,10},{10,9},{11... | collective-permute-start | bytes 294920 | tf_op jit(solution)/shard_map/ppermute | solution.py:520
  9.9 4.8 %collective-permute-start.2 = (f32[8,128]{1,0:T(8,128)S(1)}, f32[8,128]{1,0:T(8,128)S(1)}, u32[]{:S(2)}, u32[]{:S(2)}) collective-permute-start(f32[8,128]{1,0:T(8,128)S(1)} %get-tuple-element.53), channel_id=1, source_target_pairs={{0,8},{8,0},{16,24},{24,16},{1,9},{9,1},{17,25},{25,17},{2,10},{10... | collective-permute-start | bytes 12296 | tf_op jit(solution)/shard_map/ppermute | solution.py:527
  11.2 3.6 %collective-permute-start.3 = (f32[8,128]{1,0:T(8,128)S(1)}, f32[8,128]{1,0:T(8,128)S(1)}, u32[]{:S(2)}, u32[]{:S(2)}) collective-permute-start(f32[8,128]{1,0:T(8,128)S(1)} %get-tuple-element.54), channel_id=1, source_target_pairs={{8,16},{16,8},{24,0},{0,24},{9,17},{17,9},{25,1},{1,25},{10,18},{1... | collective-permute-start | bytes 12296 | tf_op jit(solution)/shard_map/ppermute | solution.py:526

commit v5 on v4

--- a/solution.py
+++ b/solution.py
@@ -98,22 +98,14 @@
 
 
 def pick_edges(slots, lanes, blocks):
-    which, lane = iota((16, lanes), 0), iota((16, lanes), 1)
-    edges = None
+    zero = jnp.zeros((1, blocks[0].shape[0]), f32)
+    edges = [zero] * 16
     for block, at in zip(blocks, slots):
-        pick = jnp.zeros((16, lanes), jnp.bool_)
+        by_lane = jnp.transpose(block)
         for deep, k in enumerate(at):
-            pick |= (which == k) & (lane == lanes - 1 - deep)
-            pick |= (which == 8 + k) & (lane == deep)
-        part = lax.dot_general(
-            jnp.where(pick, 1.0, 0.0),
-            block,
-            NT_DIMS,
-            precision=lax.Precision.HIGHEST,
-            preferred_element_type=f32,
-        )
-        edges = part if edges is None else edges + part
-    return edges
+            edges[k] = by_lane[lanes - 1 - deep : lanes - deep]
+            edges[8 + k] = by_lane[deep : deep + 1]
+    return jnp.concatenate(edges, axis=0)
 
 
 def prepare_kernel(
@@ -299,22 +291,13 @@
     for k in (0, 2):
         firsts.append(blend(ww, strip(west, k), strip(mine, 8 + k), strip(west, k + 1), up(west, k), down(west, k)))
         firsts.append(blend(we, strip(east, k), strip(east, k + 1), strip(mine, k), up(east, k), down(east, k)))
-    stack = jnp.concatenate(
-        [strip(x, k) for k in (0, 2, 6, 7) for x in (west, east)] + firsts + [jnp.zeros((4, total), f32)],
-        axis=0,
-    )
-    source, target = iota((16, 6 * lanes), 0), iota((16, 6 * lanes), 1)
-    wanted = (source // 2) * lanes + lax.rem(source, 2) * (lanes - 1)
-    rims = lax.dot_general(
-        stack,
-        jnp.where((target == wanted) & (source < 12), 1.0, 0.0),
-        TN_DIMS,
-        precision=lax.Precision.HIGHEST,
-        preferred_element_type=f32,
-    )
+    columns = [strip(x, k) for k in (0, 2, 6, 7) for x in (east, west)]
+    columns += [firsts[i] for i in (1, 0, 3, 2)]
+    stack = jnp.concatenate(columns + [jnp.zeros((lanes - len(columns), total), f32)], axis=0)
+    by_lane = jnp.transpose(stack)
     spread = (st, sq)
     cut = lambda x: x.reshape(levels, high, lanes)
-    flat = lambda i: rims[:, i * lanes : (i + 1) * lanes]
+    flat = lambda i: pltpu.roll(by_lane, lanes - 1 - 2 * i, 1)
     w = weights(cut(gx[...]), cut(gy[...]))
     full = (levels, high, lanes)
     lane, at = iota(full, 2), iota(full, 1)

time: 16.5 us -> 15.9 us (0.964)
  Pallas kernels: 10.1 us -> 9.32 us
    pallas_call x1, Pallas kernels: 0.66 us -> 0.37 us  [prepare(): pl.pallas_call(functools.partial(prepare_kernel, pad), out_shape=(HELD(t....]
    pallas_call x1, Pallas kernels: 1.63 us -> 1.38 us  [advect(): pl.pallas_call(functools.partial(advect_kernel, rows, pad), out_shape=(sh...]
    pallas_call x1, Pallas kernels: 0.33 us -> 0.12 us  [edge_columns(): pl.pallas_call(functools.partial(columns_kernel, pad), out_shape=(HELD((1...]
where the time goes in v5:
time: 15.9 us; the launch traced here: 15.7 us
  Pallas kernels  9.32 us (59%)
  starting transfers between devices  5.03 us (32%)
  between operations  1.33 us (8%)
    pallas_call x2, Pallas kernels, heating(): pl.pallas_call(functools.partial(heating_kernel, begin, end), out_shape=s...  6.41 us
    ppermute x1, starting transfers between devices, local(): lat_b = lax.ppermute(to_b, ('lon', 'lat'), odd_swaps(lat_count, lon_count))  2.47 us
    pallas_call x1, Pallas kernels, advect(): pl.pallas_call(functools.partial(advect_kernel, rows, pad), out_shape=(sh...  1.38 us
    ppermute x1, starting transfers between devices, local(): lon_a = lax.ppermute(to_a, 'lon', swaps(lon_count, 0, True))  1.29 us
    ppermute x1, starting transfers between devices, local(): lon_b = lax.ppermute(to_b, 'lon', swaps(lon_count, 1, True))  1.2 us
    pallas_call x1, Pallas kernels, edge_rows(): pl.pallas_call(functools.partial(rows_kernel, rows), out_shape=(sent, sen...  1.04 us
    pallas_call x1, Pallas kernels, prepare(): pl.pallas_call(functools.partial(prepare_kernel, pad), out_shape=(HELD(t....  0.37 us
  transfers between devices with their start and end apart: 4, of which 0 were waited for; matrix products, arithmetic and copies ran while one was open for 0% of the time, Pallas kernels for 43%

profile of v5, /device:TPU:3, one launch (start us, length us, event | category | flops | bytes accessed | tf_op | source)
XLA Modules:
  0.0 15.7 jit_solution(7717088493039011911)
XLA Ops:
  1.3 1.0 %edge_rows.1 = (f32[192,128]{1,0:T(8,128)S(1)}, f32[192,128]{1,0:T(8,128)S(1)}, s32[1,1,512]{2,1,0:T(1,128)S(1)}, f32[128,128]{1,0:T(8,128)S(1)}, f32[128,128]{1...) custom-call(s32[1,1]{1,0:T(1,128)S(6)} %copy.13.tally, ...), custom_call_target="tpu_custom_call" | custom-call | tf_op jit(solution)/shard_map/edge_rows/pallas_call | solution.py:76
  2.3 0.1 collective-permute-start
  2.4 2.5 %collective-permute-start.1 = (f32[192,128]{1,0:T(8,128)S(1)}, f32[192,128]{1,0:T(8,128)S(1)}, u32[]{:S(2)}, u32[]{:S(2)}) collective-permute-start(f32[192,128]{1,0:T(8,128)S(1)} %get-tuple-element.46), channel_id=1, source_target_pairs={{1,2},{2,1},{3,4},{4,3},{5,6},{6,5},{0,8},{7,15},{9,10},{10,9},{11... | collective-permute-start | bytes 294920 | tf_op jit(solution)/shard_map/ppermute | solution.py:503
  4.9 0.4 %prepare.1 = (f32[128,128]{1,0:T(8,128)S(1)}, bf16[256,512]{1,0:T(8,128)(2,1)S(1)}, bf16[2,112,128]{2,1,0:T(8,128)(2,1)S(1)}, bf16[3,32,16,128]{3,2,1,0:T(8,128)...) custom-call(f32[128,128]{1,0:T(8,128)S(1)} %get-tuple-element.31.t, ...), custom_call_target="tpu_custom_call" | custom-call | flops 4194304 | bytes 2097152 | tf_op jit(solution)/shard_map/prepare/pallas_call | solution.py:181
  5.2 4.0 %heating.2._.refs_0_ = f32[32,4,8,128]{3,2,1,0:T(8,128)S(1)} custom-call(bf16[256,512]{1,0:T(8,128)(2,1)S(1)} %get-tuple-element.47.linear, bf16[2,112,128]{2,1,0:T(8,128)(2,1)S(1)} %get-tuple-element.48.tables, bf16[3,32,16,128]{3,2,1,0:T(8,128)(2,1)S(1)} %get-tuple-element.49.masks, f32[112,32]{1,0:T(8,128)S(1)} %get-tuple-element.50.shares, ...), custom_call_target="tpu_custom_call" | custom-call | flops 838860800 | bytes 1048576 | tf_op jit(solution)/shard_map/heating/pallas_call | solution.py:458
  9.2 0.0 collective-permute-done.from_a.lat_a
  9.3 0.0 collective-permute-done.1.from_b.lat_b
  9.3 0.1 edge_columns.1
  9.4 1.3 %collective-permute-start.2 = (f32[8,128]{1,0:T(8,128)S(1)}, f32[8,128]{1,0:T(8,128)S(1)}, u32[]{:S(2)}, u32[]{:S(2)}) collective-permute-start(f32[8,128]{1,0:T(8,128)S(1)} %get-tuple-element.53), channel_id=1, source_target_pairs={{0,8},{8,0},{16,24},{24,16},{1,9},{9,1},{17,25},{25,17},{2,10},{10... | collective-permute-start | bytes 12296 | tf_op jit(solution)/shard_map/ppermute | solution.py:510
  10.7 1.2 %collective-permute-start.3 = (f32[8,128]{1,0:T(8,128)S(1)}, f32[8,128]{1,0:T(8,128)S(1)}, u32[]{:S(2)}, u32[]{:S(2)}) collective-permute-start(f32[8,128]{1,0:T(8,128)S(1)} %get-tuple-element.54), channel_id=1, source_target_pairs={{8,16},{16,8},{24,0},{0,24},{9,17},{17,9},{25,1},{1,25},{10,18},{1... | collective-permute-start | bytes 12296 | tf_op jit(solution)/shard_map/ppermute | solution.py:509
  11.9 2.4 %heating.3 = f32[128,128]{1,0:T(8,128)} custom-call(bf16[256,512]{1,0:T(8,128)(2,1)S(1)} %get-tuple-element.47.linear, bf16[2,112,128]{2,1,0:T(8,128)(2,1)S(1)} %get-tuple-element.48.tables, bf16[3,32,16,128]{3,2,1,0:T(8,128)(2,1)S(1)} %get-tuple-element.49.masks, f32[112,32]{1,0:T(8,128)S(1)} %get-tuple-element.50.shares, ...), custom_call_target="tpu_custom_call" | custom-call | flops 335544320 | bytes 1048576 | tf_op jit(solution)/shard_map/heating/pallas_call | solution.py:458
  14.3 0.0 collective-permute-done.2.lon_a
  14.3 0.0 collective-permute-done.3.lon_b
  14.3 1.4 %advect.1 = (f32[128,128]{1,0:T(8,128)}, f32[128,128]{1,0:T(8,128)}) custom-call(f32[256,128]{1,0:T(8,128)S(1)} %get-tuple-element.40.ft, f32[256,128]{1,0:T(8,128)S(1)} %get-tuple-element.41.fq, f32[256,128]{1,0:T(8,128)S(1)} %get-tuple-element.42.fx, f32[256,128]{1,0:T(8,128)S(1)} %get-tuple-element.43.fy, f32[16,128]{1,0:T(8,128)S(1)} %get-tuple-element.52.edges.refs_3_, ...), custom_call_target="tpu_custom_call" | custom-call | tf_op jit(solution)/shard_map/advect/pallas_call | solution.py:333
Async XLA Ops:
  2.3 6.9 %collective-permute-start = (f32[192,128]{1,0:T(8,128)S(1)}, f32[192,128]{1,0:T(8,128)S(1)}, u32[]{:S(2)}, u32[]{:S(2)}) collective-permute-start(f32[192,128]{1,0:T(8,128)S(1)} %get-tuple-element.45), channel_id=1, source_target_pairs={{0,1},{1,0},{2,3},{3,2},{4,5},{5,4},{6,7},{7,6},{8,9},{9,8},{10,11... | collective-permute-start | bytes 294920 | tf_op jit(solution)/shard_map/ppermute | solution.py:502
  2.4 6.9 %collective-permute-start.1 = (f32[192,128]{1,0:T(8,128)S(1)}, f32[192,128]{1,0:T(8,128)S(1)}, u32[]{:S(2)}, u32[]{:S(2)}) collective-permute-start(f32[192,128]{1,0:T(8,128)S(1)} %get-tuple-element.46), channel_id=1, source_target_pairs={{1,2},{2,1},{3,4},{4,3},{5,6},{6,5},{0,8},{7,15},{9,10},{10,9},{11... | collective-permute-start | bytes 294920 | tf_op jit(solution)/shard_map/ppermute | solution.py:503
  9.4 4.9 %collective-permute-start.2 = (f32[8,128]{1,0:T(8,128)S(1)}, f32[8,128]{1,0:T(8,128)S(1)}, u32[]{:S(2)}, u32[]{:S(2)}) collective-permute-start(f32[8,128]{1,0:T(8,128)S(1)} %get-tuple-element.53), channel_id=1, source_target_pairs={{0,8},{8,0},{16,24},{24,16},{1,9},{9,1},{17,25},{25,17},{2,10},{10... | collective-permute-start | bytes 12296 | tf_op jit(solution)/shard_map/ppermute | solution.py:510
  10.7 3.6 %collective-permute-start.3 = (f32[8,128]{1,0:T(8,128)S(1)}, f32[8,128]{1,0:T(8,128)S(1)}, u32[]{:S(2)}, u32[]{:S(2)}) collective-permute-start(f32[8,128]{1,0:T(8,128)S(1)} %get-tuple-element.54), channel_id=1, source_target_pairs={{8,16},{16,8},{24,0},{0,24},{9,17},{17,9},{25,1},{1,25},{10,18},{1... | collective-permute-start | bytes 12296 | tf_op jit(solution)/shard_map/ppermute | solution.py:509

commit v6 on v5

--- a/solution.py
+++ b/solution.py
@@ -343,6 +343,21 @@
 EARLY = 5
 
 
+def row_sums(tiles):
+    row = iota(tiles[0].shape, 0)
+    for far in (4, 2, 1):
+        low = (row & far) == 0
+        merged = []
+        for a, b in zip(tiles[:far], tiles[far:]):
+            other = jnp.where(low, b, a)
+            back = pltpu.roll(other, far, 0)
+            if far != 4:
+                back = jnp.where(low, pltpu.roll(other, 8 - far, 0), back)
+            merged.append(jnp.where(low, a, b) + back)
+        tiles = merged
+    return tiles[0]
+
+
 def heating_kernel(
     begin, end, linear, tables, masks, shares, albedos, *refs
 ):
@@ -377,12 +392,11 @@
             for m in range(engines):
                 pltpu.matmul_acc_lhs(at(m, l), stack)
 
-        def group(i):
+        def group(i, more=True):
             start = pl.multiple_of(i * 16, 16)
             starts = [pl.multiple_of(start + 8 * a, 8) for a in range(2)]
             w15 = [albedos[pl.ds(s, 8), :] for s in starts]
             share = [shares[pl.ds(s, 8), :] for s in starts]
-            following = jnp.minimum(i + 1, end - 1)
             y = current = step = None
             for l in range(levels):
                 if l + AHEAD < levels:
@@ -410,8 +424,8 @@
                         pull[u, l] = resist[u] * current[u]
             diffuse = [current[u] / y[u] for u in each]
             for l in range(levels - 1, -1, -1):
-                if levels - 1 - l < AHEAD:
-                    issue(following, levels - 1 - l)
+                if more and levels - 1 - l < AHEAD:
+                    issue(i + 1, levels - 1 - l)
                 if l < levels - 1:
                     diffuse = [trans[u, l] * (pull[u, l] + diffuse[u]) for u in each]
                 spread = [jnp.broadcast_to(share[a][:, l : l + 1], (8, lanes)) for a in range(2)]
@@ -430,10 +444,8 @@
             pltpu.matmul_pop(last)
         for l in range(AHEAD):
             issue(begin, l)
-        pl.loop(begin, end)(group)
-        for l in range(AHEAD):
-            for m in range(engines):
-                pltpu.matmul_pop(at(m, l))
+        pl.loop(begin, end - 1)(group)
+        group(end - 1, more=False)
 
     pl.run_scoped(
         main,
@@ -442,10 +454,12 @@
     )
     if begin == 0:
         return
-    column_scale = scale[...]
-    for l in range(levels):
-        here = pl.ds(l * rows, rows)
-        out[here, :] = jnp.sum(total[l], axis=1) * column_scale * factor[here, :]
+    block = 8 // rows
+    column_scale = jnp.concatenate([scale[...]] * block, axis=0)
+    for l in range(0, levels, block):
+        here = pl.ds(l * rows, 8)
+        sums = row_sums([total[l + i, r] for i in range(block) for r in range(rows)])
+        out[here, :] = sums * column_scale * factor[here, :]
 
 
 def heating(linear, tables, masks, shares, albedos, begin, end, more=()):

time: 15.9 us -> 15.8 us (level)
  no operation moved by 1% of the time
where the time goes in v6:
time: 15.8 us; the launch traced here: 15.7 us
  Pallas kernels  9.27 us (59%)
  starting transfers between devices  5.04 us (32%)
  between operations  1.33 us (8%)
    pallas_call x2, Pallas kernels, heating(): pl.pallas_call(functools.partial(heating_kernel, begin, end), out_shape=s...  6.36 us
    ppermute x1, starting transfers between devices, local(): lat_b = lax.ppermute(to_b, ('lon', 'lat'), odd_swaps(lat_count, lon_count))  2.47 us
    pallas_call x1, Pallas kernels, advect(): pl.pallas_call(functools.partial(advect_kernel, rows, pad), out_shape=(sh...  1.38 us
    ppermute x1, starting transfers between devices, local(): lon_a = lax.ppermute(to_a, 'lon', swaps(lon_count, 0, True))  1.29 us
    ppermute x1, starting transfers between devices, local(): lon_b = lax.ppermute(to_b, 'lon', swaps(lon_count, 1, True))  1.21 us
    pallas_call x1, Pallas kernels, edge_rows(): pl.pallas_call(functools.partial(rows_kernel, rows), out_shape=(sent, sen...  1.04 us
    pallas_call x1, Pallas kernels, prepare(): pl.pallas_call(functools.partial(prepare_kernel, pad), out_shape=(HELD(t....  0.37 us
  transfers between devices with their start and end apart: 4, of which 0 were waited for; matrix products, arithmetic and copies ran while one was open for 0% of the time, Pallas kernels for 43%

profile of v6, /device:TPU:3, one launch (start us, length us, event | category | flops | bytes accessed | tf_op | source)
XLA Modules:
  0.0 15.7 jit_solution(596317736911753771)
XLA Ops:
  1.3 1.0 %edge_rows.1 = (f32[192,128]{1,0:T(8,128)S(1)}, f32[192,128]{1,0:T(8,128)S(1)}, s32[1,1,512]{2,1,0:T(1,128)S(1)}, f32[128,128]{1,0:T(8,128)S(1)}, f32[128,128]{1...) custom-call(s32[1,1]{1,0:T(1,128)S(6)} %copy.13.tally, ...), custom_call_target="tpu_custom_call" | custom-call | tf_op jit(solution)/shard_map/edge_rows/pallas_call | solution.py:76
  2.3 0.1 collective-permute-start
  2.4 2.5 %collective-permute-start.1 = (f32[192,128]{1,0:T(8,128)S(1)}, f32[192,128]{1,0:T(8,128)S(1)}, u32[]{:S(2)}, u32[]{:S(2)}) collective-permute-start(f32[192,128]{1,0:T(8,128)S(1)} %get-tuple-element.46), channel_id=1, source_target_pairs={{1,2},{2,1},{3,4},{4,3},{5,6},{6,5},{0,8},{7,15},{9,10},{10,9},{11... | collective-permute-start | bytes 294920 | tf_op jit(solution)/shard_map/ppermute | solution.py:517
  4.9 0.4 %prepare.1 = (f32[128,128]{1,0:T(8,128)S(1)}, bf16[256,512]{1,0:T(8,128)(2,1)S(1)}, bf16[2,112,128]{2,1,0:T(8,128)(2,1)S(1)}, bf16[3,32,16,128]{3,2,1,0:T(8,128)...) custom-call(f32[128,128]{1,0:T(8,128)S(1)} %get-tuple-element.31.t, ...), custom_call_target="tpu_custom_call" | custom-call | flops 4194304 | bytes 2097152 | tf_op jit(solution)/shard_map/prepare/pallas_call | solution.py:181
  5.2 4.0 %heating.2._.refs_0_ = f32[32,4,8,128]{3,2,1,0:T(8,128)S(1)} custom-call(bf16[256,512]{1,0:T(8,128)(2,1)S(1)} %get-tuple-element.47.linear, bf16[2,112,128]{2,1,0:T(8,128)(2,1)S(1)} %get-tuple-element.48.tables, bf16[3,32,16,128]{3,2,1,0:T(8,128)(2,1)S(1)} %get-tuple-element.49.masks, f32[112,32]{1,0:T(8,128)S(1)} %get-tuple-element.50.shares, ...), custom_call_target="tpu_custom_call" | custom-call | flops 838860800 | bytes 1048576 | tf_op jit(solution)/shard_map/heating/pallas_call | solution.py:472
  9.3 0.0 collective-permute-done.from_a.lat_a
  9.3 0.0 collective-permute-done.1.from_b.lat_b
  9.3 0.1 edge_columns.1
  9.4 1.3 %collective-permute-start.2 = (f32[8,128]{1,0:T(8,128)S(1)}, f32[8,128]{1,0:T(8,128)S(1)}, u32[]{:S(2)}, u32[]{:S(2)}) collective-permute-start(f32[8,128]{1,0:T(8,128)S(1)} %get-tuple-element.53), channel_id=1, source_target_pairs={{0,8},{8,0},{16,24},{24,16},{1,9},{9,1},{17,25},{25,17},{2,10},{10... | collective-permute-start | bytes 12296 | tf_op jit(solution)/shard_map/ppermute | solution.py:524
  10.7 1.2 %collective-permute-start.3 = (f32[8,128]{1,0:T(8,128)S(1)}, f32[8,128]{1,0:T(8,128)S(1)}, u32[]{:S(2)}, u32[]{:S(2)}) collective-permute-start(f32[8,128]{1,0:T(8,128)S(1)} %get-tuple-element.54), channel_id=1, source_target_pairs={{8,16},{16,8},{24,0},{0,24},{9,17},{17,9},{25,1},{1,25},{10,18},{1... | collective-permute-start | bytes 12296 | tf_op jit(solution)/shard_map/ppermute | solution.py:523
  11.9 2.4 %heating.3 = f32[128,128]{1,0:T(8,128)} custom-call(bf16[256,512]{1,0:T(8,128)(2,1)S(1)} %get-tuple-element.47.linear, bf16[2,112,128]{2,1,0:T(8,128)(2,1)S(1)} %get-tuple-element.48.tables, bf16[3,32,16,128]{3,2,1,0:T(8,128)(2,1)S(1)} %get-tuple-element.49.masks, f32[112,32]{1,0:T(8,128)S(1)} %get-tuple-element.50.shares, ...), custom_call_target="tpu_custom_call" | custom-call | flops 335544320 | bytes 1048576 | tf_op jit(solution)/shard_map/heating/pallas_call | solution.py:472
  14.3 0.0 collective-permute-done.2.lon_a
  14.3 0.0 collective-permute-done.3.lon_b
  14.3 1.4 %advect.1 = (f32[128,128]{1,0:T(8,128)}, f32[128,128]{1,0:T(8,128)}) custom-call(f32[256,128]{1,0:T(8,128)S(1)} %get-tuple-element.40.ft, f32[256,128]{1,0:T(8,128)S(1)} %get-tuple-element.41.fq, f32[256,128]{1,0:T(8,128)S(1)} %get-tuple-element.42.fx, f32[256,128]{1,0:T(8,128)S(1)} %get-tuple-element.43.fy, f32[16,128]{1,0:T(8,128)S(1)} %get-tuple-element.52.edges.refs_3_, ...), custom_call_target="tpu_custom_call" | custom-call | tf_op jit(solution)/shard_map/advect/pallas_call | solution.py:333
Async XLA Ops:
  2.3 6.9 %collective-permute-start = (f32[192,128]{1,0:T(8,128)S(1)}, f32[192,128]{1,0:T(8,128)S(1)}, u32[]{:S(2)}, u32[]{:S(2)}) collective-permute-start(f32[192,128]{1,0:T(8,128)S(1)} %get-tuple-element.45), channel_id=1, source_target_pairs={{0,1},{1,0},{2,3},{3,2},{4,5},{5,4},{6,7},{7,6},{8,9},{9,8},{10,11... | collective-permute-start | bytes 294920 | tf_op jit(solution)/shard_map/ppermute | solution.py:516
  2.4 6.9 %collective-permute-start.1 = (f32[192,128]{1,0:T(8,128)S(1)}, f32[192,128]{1,0:T(8,128)S(1)}, u32[]{:S(2)}, u32[]{:S(2)}) collective-permute-start(f32[192,128]{1,0:T(8,128)S(1)} %get-tuple-element.46), channel_id=1, source_target_pairs={{1,2},{2,1},{3,4},{4,3},{5,6},{6,5},{0,8},{7,15},{9,10},{10,9},{11... | collective-permute-start | bytes 294920 | tf_op jit(solution)/shard_map/ppermute | solution.py:517
  9.4 4.9 %collective-permute-start.2 = (f32[8,128]{1,0:T(8,128)S(1)}, f32[8,128]{1,0:T(8,128)S(1)}, u32[]{:S(2)}, u32[]{:S(2)}) collective-permute-start(f32[8,128]{1,0:T(8,128)S(1)} %get-tuple-element.53), channel_id=1, source_target_pairs={{0,8},{8,0},{16,24},{24,16},{1,9},{9,1},{17,25},{25,17},{2,10},{10... | collective-permute-start | bytes 12296 | tf_op jit(solution)/shard_map/ppermute | solution.py:524
  10.7 3.6 %collective-permute-start.3 = (f32[8,128]{1,0:T(8,128)S(1)}, f32[8,128]{1,0:T(8,128)S(1)}, u32[]{:S(2)}, u32[]{:S(2)}) collective-permute-start(f32[8,128]{1,0:T(8,128)S(1)} %get-tuple-element.54), channel_id=1, source_target_pairs={{8,16},{16,8},{24,0},{0,24},{9,17},{17,9},{25,1},{1,25},{10,18},{1... | collective-permute-start | bytes 12296 | tf_op jit(solution)/shard_map/ppermute | solution.py:523

commit v7 on v6

--- a/solution.py
+++ b/solution.py
@@ -370,7 +370,6 @@
         so_far, factor, scale, _, out, trans, pull, beam, total = refs
     wide = 2 * lanes
     engines = rows // 2
-    total[...] = jnp.zeros_like(total) if begin == 0 else so_far[...]
     units = [(a, b) for a in range(2) for b in range(rows)]
     each = range(len(units))
 
@@ -392,7 +391,7 @@
             for m in range(engines):
                 pltpu.matmul_acc_lhs(at(m, l), stack)
 
-        def group(i, more=True):
+        def group(i, more=True, opening=False):
             start = pl.multiple_of(i * 16, 16)
             starts = [pl.multiple_of(start + 8 * a, 8) for a in range(2)]
             w15 = [albedos[pl.ds(s, 8), :] for s in starts]
@@ -434,7 +433,12 @@
                         (diffuse[a * rows + b] + beam[a * rows + b, l]) * spread[a]
                         for a in range(2)
                     ]
-                    total[l, b] = total[l, b] + (pair[0] + pair[1])
+                    both = pair[0] + pair[1]
+                    if not opening:
+                        both = total[l, b] + both
+                    elif begin > 0:
+                        both = so_far[l, b] + both
+                    total[l, b] = both
 
         nothing = jnp.zeros((16, wide), bf16)
         for m in range(engines):
@@ -444,8 +448,11 @@
             pltpu.matmul_pop(last)
         for l in range(AHEAD):
             issue(begin, l)
-        pl.loop(begin, end - 1)(group)
-        group(end - 1, more=False)
+        group(begin, more=end - begin > 1, opening=True)
+        if end - begin > 2:
+            pl.loop(begin + 1, end - 1)(group)
+        if end - begin > 1:
+            group(end - 1, more=False)
 
     pl.run_scoped(
         main,

time: 15.8 us -> 15.8 us (level)
  no operation moved by 1% of the time
where the time goes in v7:
time: 15.8 us; the launch traced here: 15.6 us
  Pallas kernels  9.25 us (59%)
  starting transfers between devices  5.04 us (32%)
  between operations  1.33 us (8%)
    pallas_call x2, Pallas kernels, heating(): pl.pallas_call(functools.partial(heating_kernel, begin, end), out_shape=s...  6.34 us
    ppermute x1, starting transfers between devices, local(): lat_b = lax.ppermute(to_b, ('lon', 'lat'), odd_swaps(lat_count, lon_count))  2.47 us
    pallas_call x1, Pallas kernels, advect(): pl.pallas_call(functools.partial(advect_kernel, rows, pad), out_shape=(sh...  1.38 us
    ppermute x1, starting transfers between devices, local(): lon_a = lax.ppermute(to_a, 'lon', swaps(lon_count, 0, True))  1.29 us
    ppermute x1, starting transfers between devices, local(): lon_b = lax.ppermute(to_b, 'lon', swaps(lon_count, 1, True))  1.21 us
    pallas_call x1, Pallas kernels, edge_rows(): pl.pallas_call(functools.partial(rows_kernel, rows), out_shape=(sent, sen...  1.04 us
    pallas_call x1, Pallas kernels, prepare(): pl.pallas_call(functools.partial(prepare_kernel, pad), out_shape=(HELD(t....  0.37 us
  transfers between devices with their start and end apart: 4, of which 0 were waited for; matrix products, arithmetic and copies ran while one was open for 0% of the time, Pallas kernels for 43%

profile of v7, /device:TPU:3, one launch (start us, length us, event | category | flops | bytes accessed | tf_op | source)
XLA Modules:
  0.0 15.6 jit_solution(3781079131726266639)
XLA Ops:
  1.3 1.0 %edge_rows.1 = (f32[192,128]{1,0:T(8,128)S(1)}, f32[192,128]{1,0:T(8,128)S(1)}, s32[1,1,512]{2,1,0:T(1,128)S(1)}, f32[128,128]{1,0:T(8,128)S(1)}, f32[128,128]{1...) custom-call(s32[1,1]{1,0:T(1,128)S(6)} %copy.13.tally, ...), custom_call_target="tpu_custom_call" | custom-call | tf_op jit(solution)/shard_map/edge_rows/pallas_call | solution.py:76
  2.3 0.1 collective-permute-start
  2.4 2.5 %collective-permute-start.1 = (f32[192,128]{1,0:T(8,128)S(1)}, f32[192,128]{1,0:T(8,128)S(1)}, u32[]{:S(2)}, u32[]{:S(2)}) collective-permute-start(f32[192,128]{1,0:T(8,128)S(1)} %get-tuple-element.46), channel_id=1, source_target_pairs={{1,2},{2,1},{3,4},{4,3},{5,6},{6,5},{0,8},{7,15},{9,10},{10,9},{11... | collective-permute-start | bytes 294920 | tf_op jit(solution)/shard_map/ppermute | solution.py:524
  4.9 0.4 %prepare.1 = (f32[128,128]{1,0:T(8,128)S(1)}, bf16[256,512]{1,0:T(8,128)(2,1)S(1)}, bf16[2,112,128]{2,1,0:T(8,128)(2,1)S(1)}, bf16[3,32,16,128]{3,2,1,0:T(8,128)...) custom-call(f32[128,128]{1,0:T(8,128)S(1)} %get-tuple-element.31.t, ...), custom_call_target="tpu_custom_call" | custom-call | flops 4194304 | bytes 2097152 | tf_op jit(solution)/shard_map/prepare/pallas_call | solution.py:181
  5.2 4.0 %heating.2._.refs_0_ = f32[32,4,8,128]{3,2,1,0:T(8,128)S(1)} custom-call(bf16[256,512]{1,0:T(8,128)(2,1)S(1)} %get-tuple-element.47.linear, bf16[2,112,128]{2,1,0:T(8,128)(2,1)S(1)} %get-tuple-element.48.tables, bf16[3,32,16,128]{3,2,1,0:T(8,128)(2,1)S(1)} %get-tuple-element.49.masks, f32[112,32]{1,0:T(8,128)S(1)} %get-tuple-element.50.shares, ...), custom_call_target="tpu_custom_call" | custom-call | flops 838860800 | bytes 1048576 | tf_op jit(solution)/shard_map/heating/pallas_call | solution.py:479
  9.2 0.0 collective-permute-done.from_a.lat_a
  9.3 0.0 collective-permute-done.1.from_b.lat_b
  9.3 0.1 edge_columns.1
  9.4 1.3 %collective-permute-start.2 = (f32[8,128]{1,0:T(8,128)S(1)}, f32[8,128]{1,0:T(8,128)S(1)}, u32[]{:S(2)}, u32[]{:S(2)}) collective-permute-start(f32[8,128]{1,0:T(8,128)S(1)} %get-tuple-element.53), channel_id=1, source_target_pairs={{0,8},{8,0},{16,24},{24,16},{1,9},{9,1},{17,25},{25,17},{2,10},{10... | collective-permute-start | bytes 12296 | tf_op jit(solution)/shard_map/ppermute | solution.py:531
  10.7 1.2 %collective-permute-start.3 = (f32[8,128]{1,0:T(8,128)S(1)}, f32[8,128]{1,0:T(8,128)S(1)}, u32[]{:S(2)}, u32[]{:S(2)}) collective-permute-start(f32[8,128]{1,0:T(8,128)S(1)} %get-tuple-element.54), channel_id=1, source_target_pairs={{8,16},{16,8},{24,0},{0,24},{9,17},{17,9},{25,1},{1,25},{10,18},{1... | collective-permute-start | bytes 12296 | tf_op jit(solution)/shard_map/ppermute | solution.py:530
  11.9 2.3 %heating.3 = f32[128,128]{1,0:T(8,128)} custom-call(bf16[256,512]{1,0:T(8,128)(2,1)S(1)} %get-tuple-element.47.linear, bf16[2,112,128]{2,1,0:T(8,128)(2,1)S(1)} %get-tuple-element.48.tables, bf16[3,32,16,128]{3,2,1,0:T(8,128)(2,1)S(1)} %get-tuple-element.49.masks, f32[112,32]{1,0:T(8,128)S(1)} %get-tuple-element.50.shares, ...), custom_call_target="tpu_custom_call" | custom-call | flops 335544320 | bytes 1048576 | tf_op jit(solution)/shard_map/heating/pallas_call | solution.py:479
  14.2 0.0 collective-permute-done.2.lon_a
  14.2 0.0 collective-permute-done.3.lon_b
  14.2 1.4 %advect.1 = (f32[128,128]{1,0:T(8,128)}, f32[128,128]{1,0:T(8,128)}) custom-call(f32[256,128]{1,0:T(8,128)S(1)} %get-tuple-element.40.ft, f32[256,128]{1,0:T(8,128)S(1)} %get-tuple-element.41.fq, f32[256,128]{1,0:T(8,128)S(1)} %get-tuple-element.42.fx, f32[256,128]{1,0:T(8,128)S(1)} %get-tuple-element.43.fy, f32[16,128]{1,0:T(8,128)S(1)} %get-tuple-element.52.edges.refs_3_, ...), custom_call_target="tpu_custom_call" | custom-call | tf_op jit(solution)/shard_map/advect/pallas_call | solution.py:333
Async XLA Ops:
  2.3 6.9 %collective-permute-start = (f32[192,128]{1,0:T(8,128)S(1)}, f32[192,128]{1,0:T(8,128)S(1)}, u32[]{:S(2)}, u32[]{:S(2)}) collective-permute-start(f32[192,128]{1,0:T(8,128)S(1)} %get-tuple-element.45), channel_id=1, source_target_pairs={{0,1},{1,0},{2,3},{3,2},{4,5},{5,4},{6,7},{7,6},{8,9},{9,8},{10,11... | collective-permute-start | bytes 294920 | tf_op jit(solution)/shard_map/ppermute | solution.py:523
  2.4 6.9 %collective-permute-start.1 = (f32[192,128]{1,0:T(8,128)S(1)}, f32[192,128]{1,0:T(8,128)S(1)}, u32[]{:S(2)}, u32[]{:S(2)}) collective-permute-start(f32[192,128]{1,0:T(8,128)S(1)} %get-tuple-element.46), channel_id=1, source_target_pairs={{1,2},{2,1},{3,4},{4,3},{5,6},{6,5},{0,8},{7,15},{9,10},{10,9},{11... | collective-permute-start | bytes 294920 | tf_op jit(solution)/shard_map/ppermute | solution.py:524
  9.4 4.8 %collective-permute-start.2 = (f32[8,128]{1,0:T(8,128)S(1)}, f32[8,128]{1,0:T(8,128)S(1)}, u32[]{:S(2)}, u32[]{:S(2)}) collective-permute-start(f32[8,128]{1,0:T(8,128)S(1)} %get-tuple-element.53), channel_id=1, source_target_pairs={{0,8},{8,0},{16,24},{24,16},{1,9},{9,1},{17,25},{25,17},{2,10},{10... | collective-permute-start | bytes 12296 | tf_op jit(solution)/shard_map/ppermute | solution.py:531
  10.7 3.6 %collective-permute-start.3 = (f32[8,128]{1,0:T(8,128)S(1)}, f32[8,128]{1,0:T(8,128)S(1)}, u32[]{:S(2)}, u32[]{:S(2)}) collective-permute-start(f32[8,128]{1,0:T(8,128)S(1)} %get-tuple-element.54), channel_id=1, source_target_pairs={{8,16},{16,8},{24,0},{0,24},{9,17},{17,9},{25,1},{1,25},{10,18},{1... | collective-permute-start | bytes 12296 | tf_op jit(solution)/shard_map/ppermute | solution.py:530
